TPU v7x, 32 devices: a whole 2x2x4 slice. The times are simulated.
32 devices in a mesh: depth: 8 (over z, y), height: 4 (over x, core).
Axes of the slice: x: 2, y: 2, z: 4, core: 2. Of those that a mesh axis runs over, the one named last changes fastest.
Arguments:
- volume: float32 [8, 64, 2048], P('height', 'depth'), may hold values from -6 to 6
- measured: float32 [16, 8, 2048], P(None, 'height', 'depth'), may hold values from -12 to 12
- taps: float32 [4, 16, 64], P(None, None, 'depth'), may hold values from 0.01 to 0.1
- band_offset: int32 [16, 8], replicated, may hold values from -64 to 64
- angle_index: int32 [16], replicated, may hold values from 0 to 719
Outputs:
- denoised: float32 [8, 64, 2048], P('height', 'depth')
Inputs may be any that keep to these rules, and one draw needn't show every extreme that they name: `band_offset`: band offsets of every angle and brick lie within plus or minus 64.
All inputs are finite; a program needn't handle non-finite values.
Results may differ from a plain program's by a relative error of at most 0.0003.
Values sent between devices are 32-bit elements; how exact they have to be, the bound alone decides.
No kernel may reach another device: no remote copies, remote signals or barrier semaphores. Data moves between devices by JAX's collectives and lax.ppermute only.
A program may use at most 64 MiB of HBM per device.

v0:
```python
import math

import jax
import jax.numpy as jnp
from jax import lax
from jax.sharding import PartitionSpec as P

TAPS = 4
OFFMAX = 64
N_VIEWS = 720
SWEEPS = 2


relax_step = 0.5
tv_step = 0.08
tv_eps = 0.1


def shifted_2(value, axis, by):
    count = lax.axis_size(axis)
    pairs = [(i, i + by) for i in range(count) if 0 <= i + by < count]
    return lax.ppermute(value, axis, pairs)


def with_halo(block, sides, width):
    for axis, dim in sides:
        count = lax.axis_size(axis)
        forward = [(i, i + 1) for i in range(count - 1)]
        backward = [(target, source) for source, target in forward]
        low = lax.ppermute(
            lax.slice_in_dim(block, block.shape[dim] - width, None, axis=dim), axis, forward
        )
        high = lax.ppermute(lax.slice_in_dim(block, 0, width, axis=dim), axis, backward)
        block = jnp.concatenate([low, block, high], axis=dim)
    return block


def cone_weights(taps, angle_index, first_slice, total_slices):
    slices = taps.shape[2]
    angle_value = 2.0 * math.pi / N_VIEWS * angle_index.astype(jnp.float32)
    depth_place = (first_slice + jnp.arange(slices, dtype=jnp.int32)).astype(jnp.float32) + 0.5
    rise = (
        0.5
        + 0.45
        * jnp.sin(angle_value)[:, None]
        * jnp.cos(math.pi / total_slices * depth_place)[None, :]
    )
    return jnp.stack([taps * (1.0 - rise)[None], taps * rise[None]], axis=2)


def binary_shift(values, amount, toward):
    length = values.shape[-1]
    for bit_number in range((2 * OFFMAX).bit_length()):
        stride = 1 << bit_number
        zero_block = jnp.zeros(values.shape[:-1] + (stride,), values.dtype)
        if toward > 0:
            shifted = jnp.concatenate([zero_block, values[..., : length - stride]], axis=-1)
        else:
            shifted = jnp.concatenate([values[..., stride:], zero_block], axis=-1)
        chosen = amount // stride % 2 == 1
        values = jnp.where(chosen, shifted, values)
    return values


def project(block, factor, offsets):
    columns = block.shape[2]
    reach = 2 * OFFMAX
    term = jnp.einsum("kasy,hyx->kashx", factor, block, precision=lax.Precision.HIGHEST)
    padded = jnp.pad(term, ((0, 0), (0, 0), (0, 0), (0, 0), (OFFMAX + TAPS, OFFMAX)))
    window = columns + reach
    summed = padded[0, ..., TAPS : TAPS + window]
    for tap_number in range(1, TAPS):
        summed = summed + padded[tap_number, ..., TAPS - tap_number : TAPS - tap_number + window]
    amount = (offsets + OFFMAX)[:, None, None, None]
    shifted = binary_shift(summed, amount, 1)[..., reach : reach + columns]
    lower = jnp.pad(shifted[:, 0], ((0, 0), (0, 1), (0, 0)))
    upper = jnp.pad(shifted[:, 1], ((0, 0), (1, 0), (0, 0)))
    return lower + upper


def backproject(extended, factor, offsets):
    columns = extended.shape[2]
    layers = extended.shape[1] - 1
    padded = jnp.pad(extended, ((0, 0), (0, 0), (OFFMAX, OFFMAX + TAPS)))
    amount = (offsets + OFFMAX)[:, None, None]
    shifted = binary_shift(padded, amount, -1)
    moved = jnp.stack(
        [shifted[..., tap_number : tap_number + columns] for tap_number in range(TAPS)], axis=0
    )
    stacked = jnp.stack([moved[:, :, :layers], moved[:, :, 1:]], axis=2)
    return jnp.einsum("kasy,kashx->hyx", factor, stacked, precision=lax.Precision.HIGHEST)


def forward(values, dimension, allowed):
    length = values.shape[dimension]
    following = jnp.concatenate(
        [
            lax.slice_in_dim(values, 1, length, axis=dimension),
            lax.slice_in_dim(values, length - 1, length, axis=dimension),
        ],
        axis=dimension,
    )
    return jnp.where(allowed, following - values, 0.0)


def backward(normal, dimension):
    length = normal.shape[dimension]
    before = jnp.concatenate(
        [
            jnp.zeros_like(lax.slice_in_dim(normal, 0, 1, axis=dimension)),
            lax.slice_in_dim(normal, 0, length - 1, axis=dimension),
        ],
        axis=dimension,
    )
    return normal - before


def allowed_mask(positions, total):
    return (positions >= 0) & (positions + 1 < total)


def tv_sweep(
    values, height_place, depth_place, width_place, height_total, depth_total, width_total
):
    along_h = forward(values, 0, allowed_mask(height_place, height_total)[:, None, None])
    along_d = forward(values, 1, allowed_mask(depth_place, depth_total)[None, :, None])
    along_w = forward(values, 2, allowed_mask(width_place, width_total)[None, None, :])
    inverse = 1.0 / jnp.sqrt(
        tv_eps * tv_eps + along_h * along_h + along_d * along_d + along_w * along_w
    )
    diverge = (
        backward(along_h * inverse, 0)
        + backward(along_d * inverse, 1)
        + backward(along_w * inverse, 2)
    )
    return values + tv_step * diverge


def margin_sweep(
    extended, depth_of, height_of, layer_count, slice_count, margin, height_total, depth_total
):
    columns = extended.shape[2]
    height_place = (
        height_of * layer_count - margin + jnp.arange(layer_count + 2 * margin, dtype=jnp.int32)
    )
    depth_place = (
        depth_of * slice_count - margin + jnp.arange(slice_count + 2 * margin, dtype=jnp.int32)
    )
    width_place = jnp.arange(columns, dtype=jnp.int32)
    return tv_sweep(
        extended, height_place, depth_place, width_place, height_total, depth_total, columns
    )


def per_device(volume, measured, taps, band_offset, angle_index):
    layer_count = volume.shape[0]
    slice_count = volume.shape[1]
    columns = volume.shape[2]
    depth_of = lax.axis_index("depth")
    height_of = lax.axis_index("height")
    depth_total = slice_count * lax.axis_size("depth")
    height_total = layer_count * lax.axis_size("height")
    band_width = columns // lax.axis_size("depth")
    factor = cone_weights(taps, angle_index, depth_of * slice_count, depth_total)
    offsets = lax.dynamic_slice_in_dim(band_offset, depth_of, 1, 1)[:, 0]
    partial_value = project(volume, factor, offsets)
    spill = shifted_2(partial_value[:, layer_count], "height", 1)
    own = partial_value[:, :layer_count].at[:, 0].add(spill)
    placed = lax.dynamic_update_slice_in_dim(
        jnp.zeros_like(own), measured, depth_of * band_width, 2
    )
    whole = -lax.psum(own - placed, "depth")
    upper = shifted_2(whole[:, 0], "height", -1)
    extended = jnp.concatenate([whole, upper[:, None]], axis=1)
    update = backproject(extended, factor, offsets)
    values = volume + relax_step * update
    for sweep_index in range(SWEEPS):
        widened = with_halo(values, (("depth", 1), ("height", 0)), 1)
        widened = margin_sweep(
            widened, depth_of, height_of, layer_count, slice_count, 1, height_total, depth_total
        )
        values = widened[1:-1, 1:-1]
    return values


def solution(mesh):
    in_specs = (
        P("height", "depth", None),
        P(None, "height", "depth"),
        P(None, None, "depth"),
        P(),
        P(),
    )
    out_specs = P("height", "depth", None)
    return jax.shard_map(
        per_device, mesh=mesh, in_specs=in_specs, out_specs=out_specs, check_vma=False
    )
```

profile of v0, /device:TPU:1, one launch (start us, length us, event | category | flops | bytes accessed | tf_op | source)
XLA Modules:
  0.0 152.3 jit_solution(4609843290849259998)
XLA Ops:
  7.4 0.7 multiply_bitcast_fusion.1
  8.1 2.8 %fusion.25 = f32[4,16,2,2,2048]{4,1,3,2,0:T(8,128)S(1)} fusion(f32[2,8,2048]{2,1,0:T(8,128)} %param.7, f32[4,16,1,8]{1,3,2,0:T(8,128)S(1)} %get-tuple-element.46, f32[4,16,1,8]{1,3,2,0:T(8,128)S(1)} %get-tuple-element.45), kind=kOutput, calls=%fused_computation.82 | convolution fusion | flops 50332672 | bytes 2232320 | tf_op jit(solution)/shard_map/kasy,hyx->kashx/dot_general | solution.py:68
  12.3 0.8 pad_select_fusion.7
  14.6 4.5 %collective-permute-start = (f32[16,2048]{1,0:T(8,128)S(1)}, f32[16,2048]{1,0:T(8,128)S(1)}, u32[]{:S(2)}, u32[]{:S(2)}) collective-permute-start(f32[16,2048]{1,0:T(8,128)S(1)} %fusion.24), channel_id=1, source_target_pairs={{0,1},{1,2},{2,3},{4,5},{5,6},{6,7},{8,9},{9,10},{10,11},{12,13},{... | collective-permute-start | bytes 393224 | tf_op jit(solution)/shard_map/ppermute | solution.py:22
  19.2 1.8 %collective-permute-done = f32[16,2048]{1,0:T(8,128)S(1)} collective-permute-done((f32[16,2048]{1,0:T(8,128)S(1)}, f32[16,2048]{1,0:T(8,128)S(1)}, u32[]{:S(2)}, u32[]{:S(2)}) %collective-permute-start) | collective-permute-done | bytes 131104 | tf_op jit(solution)/shard_map/ppermute | solution.py:22
  21.1 0.7 sub.98
  21.8 71.2 %all-reduce.28.cloned.1.call-done = f32[16,2,2048]{2,0,1:T(8,128)} async-done(((f32[16,2,2048]{2,0,1:T(8,128)}), f32[16,2,2048]{2,0,1:T(8,128)}) %all-reduce.28.cloned.1.call-update) | async-done | bytes 262160 | tf_op jit(solution)/shard_map/psum | solution.py:172
  93.1 1.0 neg.3
  94.1 4.4 %collective-permute-start.1 = (f32[16,2048]{1,0:T(8,128)S(1)}, f32[16,2048]{1,0:T(8,128)S(1)}, u32[]{:S(2)}, u32[]{:S(2)}) collective-permute-start(f32[16,2048]{1,0:T(8,128)S(1)} %slice_bitcast_fusion.8), channel_id=1, source_target_pairs={{1,0},{2,1},{3,2},{5,4},{6,5},{7,6},{9,8},{10,9},{11,10},{13,12},{... | collective-permute-start | bytes 393224 | tf_op jit(solution)/shard_map/ppermute | solution.py:22
  98.5 3.7 %collective-permute-done.1 = f32[16,2048]{1,0:T(8,128)S(1)} collective-permute-done((f32[16,2048]{1,0:T(8,128)S(1)}, f32[16,2048]{1,0:T(8,128)S(1)}, u32[]{:S(2)}, u32[]{:S(2)}) %collective-permute-start.1) | collective-permute-done | bytes 131104 | tf_op jit(solution)/shard_map/ppermute | solution.py:22
  106.0 1.2 fusion.2
  107.3 2.3 %collective-permute-start.2 = (f32[2,1,2048]{2,1,0:T(1,128)S(1)}, f32[2,1,2048]{2,1,0:T(1,128)S(1)}, u32[]{:S(2)}, u32[]{:S(2)}) collective-permute-start(f32[2,1,2048]{2,1,0:T(1,128)S(1)} %get-tuple-element.43), channel_id=1, source_target_pairs={{0,4},{4,8},{8,12},{12,16},{16,20},{20,24},{24,28},{1,5},{5,9},{9,... | collective-permute-start | bytes 49160 | tf_op jit(solution)/shard_map/ppermute | solution.py:30
  109.6 1.3 collective-permute-start.3
  110.9 3.2 %collective-permute-done.3 = f32[2,1,2048]{2,1,0:T(1,128)S(1)} collective-permute-done((f32[2,1,2048]{2,1,0:T(1,128)S(1)}, f32[2,1,2048]{2,1,0:T(1,128)S(1)}, u32[]{:S(2)}, u32[]{:S(2)}) %collective-permute-start.3) | collective-permute-done | bytes 16416 | tf_op jit(solution)/shard_map/ppermute | solution.py:33
  114.2 3.2 %collective-permute-start.4 = (f32[1,10,2048]{2,1,0:T(8,128)S(1)}, f32[1,10,2048]{2,1,0:T(8,128)S(1)}, u32[]{:S(2)}, u32[]{:S(2)}) collective-permute-start(f32[1,10,2048]{2,1,0:T(8,128)S(1)} %get-tuple-element.41), channel_id=1, source_target_pairs={{0,1},{1,2},{2,3},{4,5},{5,6},{6,7},{8,9},{9,10},{10,11},{12,13},{... | collective-permute-start | bytes 245768 | tf_op jit(solution)/shard_map/ppermute | solution.py:30
  117.4 1.9 %collective-permute-start.5 = (f32[1,10,2048]{2,1,0:T(8,128)S(1)}, f32[1,10,2048]{2,1,0:T(8,128)S(1)}, u32[]{:S(2)}, u32[]{:S(2)}) collective-permute-start(f32[1,10,2048]{2,1,0:T(8,128)S(1)} %get-tuple-element.42), channel_id=1, source_target_pairs={{1,0},{2,1},{3,2},{5,4},{6,5},{7,6},{9,8},{10,9},{11,10},{13,12},{... | collective-permute-start | bytes 245768 | tf_op jit(solution)/shard_map/ppermute | solution.py:33
  119.3 4.3 %collective-permute-done.5 = f32[1,10,2048]{2,1,0:T(8,128)S(1)} collective-permute-done((f32[1,10,2048]{2,1,0:T(8,128)S(1)}, f32[1,10,2048]{2,1,0:T(8,128)S(1)}, u32[]{:S(2)}, u32[]{:S(2)}) %collective-permute-start.5) | collective-permute-done | bytes 81952 | tf_op jit(solution)/shard_map/ppermute | solution.py:33
  125.2 4.3 %collective-permute-start.6 = (f32[2,1,2048]{2,1,0:T(1,128)S(1)}, f32[2,1,2048]{2,1,0:T(1,128)S(1)}, u32[]{:S(2)}, u32[]{:S(2)}) collective-permute-start(f32[2,1,2048]{2,1,0:T(1,128)S(1)} %get-tuple-element.33), channel_id=1, source_target_pairs={{0,4},{4,8},{8,12},{12,16},{16,20},{20,24},{24,28},{1,5},{5,9},{9,... | collective-permute-start | bytes 49160 | tf_op jit(solution)/shard_map/ppermute | solution.py:30
  129.5 1.3 collective-permute-start.7
  130.8 3.1 %collective-permute-done.7 = f32[2,1,2048]{2,1,0:T(1,128)S(1)} collective-permute-done((f32[2,1,2048]{2,1,0:T(1,128)S(1)}, f32[2,1,2048]{2,1,0:T(1,128)S(1)}, u32[]{:S(2)}, u32[]{:S(2)}) %collective-permute-start.7) | collective-permute-done | bytes 16416 | tf_op jit(solution)/shard_map/ppermute | solution.py:33
  134.0 3.2 %collective-permute-start.8 = (f32[1,10,2048]{2,1,0:T(8,128)S(1)}, f32[1,10,2048]{2,1,0:T(8,128)S(1)}, u32[]{:S(2)}, u32[]{:S(2)}) collective-permute-start(f32[1,10,2048]{2,1,0:T(8,128)S(1)} %get-tuple-element.39), channel_id=1, source_target_pairs={{0,1},{1,2},{2,3},{4,5},{5,6},{6,7},{8,9},{9,10},{10,11},{12,13},{... | collective-permute-start | bytes 245768 | tf_op jit(solution)/shard_map/ppermute | solution.py:30
  137.2 1.9 %collective-permute-start.9 = (f32[1,10,2048]{2,1,0:T(8,128)S(1)}, f32[1,10,2048]{2,1,0:T(8,128)S(1)}, u32[]{:S(2)}, u32[]{:S(2)}) collective-permute-start(f32[1,10,2048]{2,1,0:T(8,128)S(1)} %get-tuple-element.40), channel_id=1, source_target_pairs={{1,0},{2,1},{3,2},{5,4},{6,5},{7,6},{9,8},{10,9},{11,10},{13,12},{... | collective-permute-start | bytes 245768 | tf_op jit(solution)/shard_map/ppermute | solution.py:33
  139.2 4.3 %collective-permute-done.9 = f32[1,10,2048]{2,1,0:T(8,128)S(1)} collective-permute-done((f32[1,10,2048]{2,1,0:T(8,128)S(1)}, f32[1,10,2048]{2,1,0:T(8,128)S(1)}, u32[]{:S(2)}, u32[]{:S(2)}) %collective-permute-start.9) | collective-permute-done | bytes 81952 | tf_op jit(solution)/shard_map/ppermute | solution.py:33
  144.6 0.8 slice_add_fusion
  (78 shorter events, 10.3 us)
Async XLA Ops:
  6.5 86.5 %all-reduce.28.cloned.1.call-start = ((), (), s32[]{:S(2)}) async-start(), calls=%async_computation | async-start | bytes 524288 | tf_op jit(solution)/shard_map/psum | solution.py:172
  14.4 4.8 %copy-start.1 = (f32[16,2,256]{2,1,0:T(2,128)S(1)}, f32[16,2,256]{2,1,0:T(2,128)}, u32[]{:S(2)}) copy-start(f32[16,2,256]{2,1,0:T(2,128)} %param.8) | copy-start | bytes 98308
  14.6 6.4 %collective-permute-start = (f32[16,2048]{1,0:T(8,128)S(1)}, f32[16,2048]{1,0:T(8,128)S(1)}, u32[]{:S(2)}, u32[]{:S(2)}) collective-permute-start(f32[16,2048]{1,0:T(8,128)S(1)} %fusion.24), channel_id=1, source_target_pairs={{0,1},{1,2},{2,3},{4,5},{5,6},{6,7},{8,9},{9,10},{10,11},{12,13},{... | collective-permute-start | bytes 393224 | tf_op jit(solution)/shard_map/ppermute | solution.py:22
  94.1 8.1 %collective-permute-start.1 = (f32[16,2048]{1,0:T(8,128)S(1)}, f32[16,2048]{1,0:T(8,128)S(1)}, u32[]{:S(2)}, u32[]{:S(2)}) collective-permute-start(f32[16,2048]{1,0:T(8,128)S(1)} %slice_bitcast_fusion.8), channel_id=1, source_target_pairs={{1,0},{2,1},{3,2},{5,4},{6,5},{7,6},{9,8},{10,9},{11,10},{13,12},{... | collective-permute-start | bytes 393224 | tf_op jit(solution)/shard_map/ppermute | solution.py:22
  105.1 0.9 copy-start
  107.3 3.6 %collective-permute-start.2 = (f32[2,1,2048]{2,1,0:T(1,128)S(1)}, f32[2,1,2048]{2,1,0:T(1,128)S(1)}, u32[]{:S(2)}, u32[]{:S(2)}) collective-permute-start(f32[2,1,2048]{2,1,0:T(1,128)S(1)} %get-tuple-element.43), channel_id=1, source_target_pairs={{0,4},{4,8},{8,12},{12,16},{16,20},{20,24},{24,28},{1,5},{5,9},{9,... | collective-permute-start | bytes 49160 | tf_op jit(solution)/shard_map/ppermute | solution.py:30
  109.6 4.5 %collective-permute-start.3 = (f32[2,1,2048]{2,1,0:T(1,128)S(1)}, f32[2,1,2048]{2,1,0:T(1,128)S(1)}, u32[]{:S(2)}, u32[]{:S(2)}) collective-permute-start(f32[2,1,2048]{2,1,0:T(1,128)S(1)} %get-tuple-element.44), channel_id=1, source_target_pairs={{4,0},{8,4},{12,8},{16,12},{20,16},{24,20},{28,24},{5,1},{9,5},{13... | collective-permute-start | bytes 49160 | tf_op jit(solution)/shard_map/ppermute | solution.py:33
  114.2 5.1 %collective-permute-start.4 = (f32[1,10,2048]{2,1,0:T(8,128)S(1)}, f32[1,10,2048]{2,1,0:T(8,128)S(1)}, u32[]{:S(2)}, u32[]{:S(2)}) collective-permute-start(f32[1,10,2048]{2,1,0:T(8,128)S(1)} %get-tuple-element.41), channel_id=1, source_target_pairs={{0,1},{1,2},{2,3},{4,5},{5,6},{6,7},{8,9},{9,10},{10,11},{12,13},{... | collective-permute-start | bytes 245768 | tf_op jit(solution)/shard_map/ppermute | solution.py:30
  117.4 6.3 %collective-permute-start.5 = (f32[1,10,2048]{2,1,0:T(8,128)S(1)}, f32[1,10,2048]{2,1,0:T(8,128)S(1)}, u32[]{:S(2)}, u32[]{:S(2)}) collective-permute-start(f32[1,10,2048]{2,1,0:T(8,128)S(1)} %get-tuple-element.42), channel_id=1, source_target_pairs={{1,0},{2,1},{3,2},{5,4},{6,5},{7,6},{9,8},{10,9},{11,10},{13,12},{... | collective-permute-start | bytes 245768 | tf_op jit(solution)/shard_map/ppermute | solution.py:33
  125.2 5.6 %collective-permute-start.6 = (f32[2,1,2048]{2,1,0:T(1,128)S(1)}, f32[2,1,2048]{2,1,0:T(1,128)S(1)}, u32[]{:S(2)}, u32[]{:S(2)}) collective-permute-start(f32[2,1,2048]{2,1,0:T(1,128)S(1)} %get-tuple-element.33), channel_id=1, source_target_pairs={{0,4},{4,8},{8,12},{12,16},{16,20},{20,24},{24,28},{1,5},{5,9},{9,... | collective-permute-start | bytes 49160 | tf_op jit(solution)/shard_map/ppermute | solution.py:30
  129.5 4.5 %collective-permute-start.7 = (f32[2,1,2048]{2,1,0:T(1,128)S(1)}, f32[2,1,2048]{2,1,0:T(1,128)S(1)}, u32[]{:S(2)}, u32[]{:S(2)}) collective-permute-start(f32[2,1,2048]{2,1,0:T(1,128)S(1)} %get-tuple-element.34), channel_id=1, source_target_pairs={{4,0},{8,4},{12,8},{16,12},{20,16},{24,20},{28,24},{5,1},{9,5},{13... | collective-permute-start | bytes 49160 | tf_op jit(solution)/shard_map/ppermute | solution.py:33
  134.0 5.2 %collective-permute-start.8 = (f32[1,10,2048]{2,1,0:T(8,128)S(1)}, f32[1,10,2048]{2,1,0:T(8,128)S(1)}, u32[]{:S(2)}, u32[]{:S(2)}) collective-permute-start(f32[1,10,2048]{2,1,0:T(8,128)S(1)} %get-tuple-element.39), channel_id=1, source_target_pairs={{0,1},{1,2},{2,3},{4,5},{5,6},{6,7},{8,9},{9,10},{10,11},{12,13},{... | collective-permute-start | bytes 245768 | tf_op jit(solution)/shard_map/ppermute | solution.py:30
  137.2 6.3 %collective-permute-start.9 = (f32[1,10,2048]{2,1,0:T(8,128)S(1)}, f32[1,10,2048]{2,1,0:T(8,128)S(1)}, u32[]{:S(2)}, u32[]{:S(2)}) collective-permute-start(f32[1,10,2048]{2,1,0:T(8,128)S(1)} %get-tuple-element.40), channel_id=1, source_target_pairs={{1,0},{2,1},{3,2},{5,4},{6,5},{7,6},{9,8},{10,9},{11,10},{13,12},{... | collective-permute-start | bytes 245768 | tf_op jit(solution)/shard_map/ppermute | solution.py:33
Sparse Core Ops, SparseCore 0:
  22.0 71.0 all-reduce.27
where the time goes:
time: 153 us; the launch traced here: 152 us
  waiting for transfers between devices  91.8 us (60%)
  starting transfers between devices  28.3 us (18%)
  between operations  13.9 us (9%)
  other arithmetic  10.8 us (7%)
  matrix products  3.96 us (3%)
  local copies, waits for them, and re-layouts  3.5 us (2%)
    psum x1, waiting for transfers between devices, per_device(): whole = -lax.psum(own - placed, 'depth')  71.2 us
    ppermute x4, waiting for transfers between devices, with_halo(): lax.ppermute(lax.slice_in_dim(block, 0, width, axis=dim), axis, backward)  15 us
    ppermute x4, starting transfers between devices, with_halo(): lax.ppermute(lax.slice_in_dim(block, block.shape[dim] - width, None, axis...  13 us
    ppermute x2, starting transfers between devices, shifted_2(): return lax.ppermute(value, axis, pairs)  8.92 us
    ppermute x4, starting transfers between devices, with_halo(): lax.ppermute(lax.slice_in_dim(block, 0, width, axis=dim), axis, backward)  6.43 us
    ppermute x2, waiting for transfers between devices, shifted_2(): return lax.ppermute(value, axis, pairs)  5.53 us
    select_n x16, other arithmetic, binary_shift(): values = jnp.where(chosen, shifted, values)  3.12 us
  transfers between devices with their start and end apart: 11, of which 7 were waited for; matrix products, arithmetic and copies ran while one was open for 0% of the time, Pallas kernels for 0%

commit v1 on v0

v1 whole, which is shorter than its diff:
```python
import math

import jax
import jax.numpy as jnp
from jax import lax
from jax.experimental import pallas as pl
from jax.experimental.pallas import tpu as pltpu
from jax.sharding import PartitionSpec as P

OFFMAX = 64
N_VIEWS = 720
SWEEPS = 2
LANES = 128
SUB = 8

relax_step = 0.5
tv_step = 0.08
tv_eps = 0.1

VMEM = pl.BlockSpec(memory_space=pltpu.VMEM)
SMEM = pl.BlockSpec(memory_space=pltpu.SMEM)


def up_to(value, unit):
    return -(-value // unit) * unit


class Sizes:
    def __init__(self, volume, measured, taps, depth_count, height_count):
        self.depth, self.height = depth_count, height_count
        self.layers, self.slices, self.columns = volume.shape
        self.taps, self.angles = taps.shape[:2]
        self.band = self.columns // depth_count
        self.total_slices = self.slices * depth_count
        self.left = OFFMAX + SWEEPS
        self.width = self.band + 2 * SWEEPS + 2 * OFFMAX + self.taps - 1
        self.vol_left = self.left + OFFMAX + self.taps - 1
        self.vol_width = self.width + 2 * OFFMAX + self.taps - 1
        self.field = self.band + 2 * SWEEPS
        self.width_p = up_to(self.width, LANES)
        self.vol_p = up_to(self.vol_width, LANES)
        self.field_p = up_to(self.field + self.taps - 1, LANES)
        self.pieces = []
        for away in range(-depth_count + 1, depth_count):
            first = max(0, away * self.band - self.left)
            last = min(self.band, self.width + away * self.band - self.left)
            if last > first:
                self.pieces.append((away, first, last))
        self.reach = max(abs(piece[0]) for piece in self.pieces)
        self.piece_p = max(
            [last - first for away, first, last in self.pieces if away != 0] + [1]
        )
        self.tap_lanes = self.taps * self.slices
        self.aligned = self.vol_width // LANES * LANES
        self.tap_at = self.vol_width - self.aligned
        self.piece_at = self.tap_at + self.tap_lanes
        self.message = up_to(
            self.vol_width + self.tap_lanes + self.layers * self.piece_p, LANES
        )
        self.extra = self.message - self.aligned
        self.rows = self.layers * self.slices


def lane_index(shape):
    return lax.broadcasted_iota(jnp.int32, shape, len(shape) - 1)


def roll_left(value, amount):
    width = value.shape[-1]
    amount = amount % width
    return value if amount == 0 else pltpu.roll(value, width - amount, value.ndim - 1)


def split(value):
    high = value.astype(jnp.bfloat16).astype(jnp.float32)
    return high, value - high


def pack_kernel(z, me_ref, volume_ref, extra_ref, out_ref):
    front = up_to(z.vol_left, LANES)
    back = up_to(z.vol_p + LANES, LANES)
    padded = jnp.concatenate(
        [
            jnp.zeros((z.rows, front), jnp.float32),
            volume_ref[...],
            jnp.zeros((z.rows, back), jnp.float32),
        ],
        axis=1,
    )
    me = me_ref[0]
    rolled = {}
    lane = lane_index((z.rows, LANES))
    for target in range(z.depth):
        start = front + target * z.band - z.vol_left
        shift = start % LANES
        if shift not in rolled:
            rolled[shift] = roll_left(padded, shift)
        begin = start - shift
        out_ref[target, :, : z.aligned] = rolled[shift][:, begin : begin + z.aligned]
        away = jnp.clip(target - me, -z.reach, z.reach) + z.reach
        extra = extra_ref[away]
        tail = rolled[shift][:, begin + z.aligned : begin + z.aligned + LANES]
        out_ref[target, :, z.aligned : z.aligned + LANES] = jnp.where(
            lane < z.tap_at, tail, extra[:, :LANES]
        )
        if z.extra > LANES:
            out_ref[target, :, z.aligned + LANES :] = extra[:, LANES:]


def tap_rows(z, message_ref, brick):
    tile = roll_left(
        message_ref[brick, : z.angles, z.aligned : z.aligned + LANES], z.tap_at
    )
    tile = jnp.where(lane_index(tile.shape) < z.tap_lanes, tile, 0.0)
    period = z.tap_lanes
    while period < LANES:
        tile = tile + pltpu.roll(tile, period, 1)
        period *= 2
    return tile


def spread_rows(z, low, high):
    width = low.shape[1]
    layer = lane_index((SUB, width)) % (z.layers * z.tap_lanes) // z.tap_lanes
    row = lax.broadcasted_iota(jnp.int32, (SUB, width), 0)
    same, above = row == layer, row == layer + 1
    blocks = []
    for angle in range(z.angles):
        first = jnp.broadcast_to(low[angle : angle + 1], (SUB, width))
        second = jnp.broadcast_to(high[angle : angle + 1], (SUB, width))
        blocks.append(jnp.where(same, first, jnp.where(above, second, 0.0)))
    return jnp.concatenate(blocks, axis=0)


def project_kernel(z, me_ref, offset_ref, message_ref, own_ref, sine_ref, cosine_ref, out_ref, sum_ref):
    me = me_ref[0]
    inner = z.layers * z.tap_lanes
    segment_lanes = up_to(3 * inner, LANES)
    sum_ref[...] = jnp.zeros_like(sum_ref)

    def brick_step(brick, carry):
        taps = tap_rows(z, message_ref, brick)
        taps = jnp.concatenate([taps] * (segment_lanes // LANES), axis=1)
        rise = 0.5 + 0.45 * sine_ref[...] * cosine_ref[brick]
        middle = lane_index(taps.shape) // inner == 1
        parts = []
        for weight in (taps * (1.0 - rise), taps * rise):
            high, low = split(weight)
            parts.append(jnp.where(middle, low, high))
        left = spread_rows(z, parts[0], parts[1])[:, : 3 * inner].astype(jnp.bfloat16)
        highs, lows = [], []
        for layer in range(z.layers):
            block = message_ref[brick, layer * z.slices : (layer + 1) * z.slices, : z.vol_p]
            high, low = split(block)
            for tap in range(z.taps):
                highs.append(pltpu.roll(high, tap, 1) if tap else high)
                lows.append(pltpu.roll(low, tap, 1) if tap else low)
        high = jnp.concatenate(highs, axis=0).astype(jnp.bfloat16)
        low = jnp.concatenate(lows, axis=0).astype(jnp.bfloat16)
        product = jnp.dot(
            left,
            jnp.concatenate([high, high, low], axis=0),
            preferred_element_type=jnp.float32,
        )
        for angle in range(z.angles):
            amount = z.vol_p - (OFFMAX + z.taps - 1) + offset_ref[angle, brick]
            moved = pltpu.roll(product[angle * SUB : (angle + 1) * SUB], amount, 1)
            for tile in range(z.width_p // LANES):
                rows = pl.ds((tile * z.angles + angle) * SUB, SUB)
                sum_ref[rows, :] = sum_ref[rows, :] + moved[:, tile * LANES : (tile + 1) * LANES]
        return carry

    lax.fori_loop(0, z.depth, brick_step, 0)
    lane = lane_index((z.angles, z.width_p))
    column = me * z.band - z.left + lane
    inside = (column >= 0) & (column < z.columns)
    for row in range(z.layers + 1):
        total = -jnp.concatenate(
            [
                sum_ref[pl.ds(tile * z.angles * SUB + row, z.angles, SUB), :]
                for tile in range(z.width_p // LANES)
            ],
            axis=1,
        )
        if row < z.layers:
            window = own_ref[row]
            for away, first, last in z.pieces:
                if away == 0:
                    continue
                source = jnp.clip(me - away, 0, z.depth - 1)
                tail = message_ref[source, : z.angles, z.aligned :]
                if z.extra < z.width_p:
                    tail = jnp.concatenate(
                        [tail, jnp.zeros((z.angles, z.width_p - z.extra), jnp.float32)], axis=1
                    )
                else:
                    tail = tail[:, : z.width_p]
                begin = first - away * z.band + z.left
                tail = roll_left(tail, z.piece_at + row * z.piece_p - begin)
                here = (lane >= begin) & (lane < begin + last - first)
                window = jnp.where(here, tail, window)
            total = total + window
        out_ref[row] = jnp.where(inside, total, 0.0)


def adjoint_kernel(z, message_ref, sine_ref, cosine_ref, out_ref):
    inner = z.layers * z.tap_lanes

    def brick_step(brick, carry):
        taps = tap_rows(z, message_ref, brick)
        rise = 0.5 + 0.45 * sine_ref[:, :LANES] * cosine_ref[brick, :, :LANES]
        spread = spread_rows(z, taps * (1.0 - rise), taps * rise)
        high, low = split(spread.T[:inner])
        out_ref[brick] = jnp.concatenate([high, low, high], axis=1).astype(jnp.bfloat16)
        return carry

    lax.fori_loop(0, z.depth, brick_step, 0)


def backproject_kernel(z, place_ref, offset_ref, own_ref, below_ref, above_ref, message_ref, weight_ref, out_ref, row_ref):
    row_ref[...] = jnp.zeros_like(row_ref)
    last = place_ref[1] == z.height - 1
    for row in range(z.layers + 1):
        value = own_ref[row]
        if row == 0:
            value = value + below_ref[...]
        if row == z.layers:
            value = jnp.where(last, 0.0, value + above_ref[...])
        for tile in range(z.width_p // LANES):
            row_ref[pl.ds(tile * z.angles * SUB + row, z.angles, SUB), :] = value[
                :, tile * LANES : (tile + 1) * LANES
            ]
    lead = z.vol_left - SWEEPS

    def brick_step(brick, carry):
        blocks = []
        for angle in range(z.angles):
            amount = (z.width_p - OFFMAX - offset_ref[angle, brick]) % z.width_p
            block = jnp.concatenate(
                [
                    row_ref[pl.ds((tile * z.angles + angle) * SUB, SUB), :]
                    for tile in range(z.width_p // LANES)
                ],
                axis=1,
            )
            block = pltpu.roll(block, amount, 1)
            blocks.append(block[:, : z.field_p])
        high, low = split(jnp.concatenate(blocks, axis=0))
        high = high.astype(jnp.bfloat16)
        low = low.astype(jnp.bfloat16)
        product = jnp.dot(
            weight_ref[brick],
            jnp.concatenate([high, high, low], axis=0),
            preferred_element_type=jnp.float32,
        )
        for layer in range(z.layers):
            update = None
            for tap in range(z.taps):
                begin = (layer * z.taps + tap) * z.slices
                term = roll_left(product[begin : begin + z.slices], tap)
                update = term if update is None else update + term
            start = lead // LANES * LANES
            voxels = message_ref[
                brick, layer * z.slices : (layer + 1) * z.slices, start : start + z.field_p + LANES
            ]
            voxels = roll_left(voxels, lead - start)[:, : z.field_p]
            out_ref[layer, brick] = voxels + relax_step * update
        return carry

    lax.fori_loop(0, z.depth, brick_step, 0)


def denoise_kernel(z, place_ref, below_ref, own_ref, above_ref, out_ref):
    shape = (z.total_slices, z.field_p)
    column = place_ref[0] * z.band - SWEEPS + lane_index(shape)
    slice_at = lax.broadcasted_iota(jnp.int32, shape, 0)
    allow_x = (column >= 0) & (column + 1 < z.columns)
    allow_y = slice_at + 1 < z.total_slices
    not_first = slice_at > 0
    first_layer = place_ref[1] * z.layers
    values = {}
    for layer in range(-SWEEPS, z.layers + SWEEPS):
        if layer < 0:
            values[layer] = below_ref[z.layers + layer]
        elif layer < z.layers:
            values[layer] = own_ref[layer]
        else:
            values[layer] = above_ref[layer - z.layers]
    for sweep in range(SWEEPS):
        margin = SWEEPS - 1 - sweep
        later = {}
        before = None
        for layer in range(-margin - 1, z.layers + margin):
            here = values[layer]
            place = first_layer + layer
            allow_z = (place >= 0) & (place + 1 < z.height * z.layers)
            along_z = jnp.where(allow_z, values[layer + 1] - here, 0.0)
            along_y = jnp.where(allow_y, pltpu.roll(here, z.total_slices - 1, 0) - here, 0.0)
            along_x = jnp.where(allow_x, roll_left(here, 1) - here, 0.0)
            inverse = lax.rsqrt(
                tv_eps * tv_eps + along_z * along_z + along_y * along_y + along_x * along_x
            )
            normal_z = along_z * inverse
            if layer >= -margin:
                normal_y = along_y * inverse
                normal_x = along_x * inverse
                diverge = (
                    normal_z
                    - before
                    + normal_y
                    - jnp.where(not_first, pltpu.roll(normal_y, 1, 0), 0.0)
                    + normal_x
                    - pltpu.roll(normal_x, 1, 1)
                )
                later[layer] = here + tv_step * diverge
            before = normal_z
        values = later
    for layer in range(z.layers):
        result = roll_left(values[layer], SWEEPS)
        for brick in range(z.depth):
            out_ref[brick, layer] = result[brick * z.slices : (brick + 1) * z.slices, : z.band]


def shifted(value, axis, by):
    count = lax.axis_size(axis)
    pairs = [(i, i + by) for i in range(count) if 0 <= i + by < count]
    return lax.ppermute(value, axis, pairs)


def call(kernel, z, shape, specs, scratch=(), dtype=jnp.float32, cycles=2000):
    return pl.pallas_call(
        lambda *refs: kernel(z, *refs),
        out_shape=jax.ShapeDtypeStruct(shape, dtype),
        in_specs=specs,
        out_specs=VMEM,
        scratch_shapes=list(scratch),
        name=kernel.__name__,
    )


def per_device(volume, measured, taps, band_offset, angle_index):
    z = Sizes(volume, measured, taps, lax.axis_size("depth"), lax.axis_size("height"))
    depth_of = lax.axis_index("depth")
    height_of = lax.axis_index("height")
    place = jnp.stack([depth_of, height_of]).astype(jnp.int32)

    tap_part = jnp.transpose(taps, (1, 0, 2)).reshape(z.angles, z.tap_lanes)
    extras = []
    table = {away: (first, last) for away, first, last in z.pieces}
    for away in range(-z.reach, z.reach + 1):
        parts = [jnp.zeros((z.angles, z.tap_at), jnp.float32), tap_part]
        for row in range(z.layers):
            first, last = table[away] if away != 0 else (0, 0)
            piece = measured[:, row, first:last]
            parts.append(jnp.pad(piece, ((0, 0), (0, z.piece_p - (last - first)))))
        joined = jnp.concatenate(parts, axis=1)
        extras.append(jnp.pad(joined, ((0, z.rows - z.angles), (0, z.extra - joined.shape[1]))))
    extra = jnp.stack(extras)
    own = jnp.pad(
        jnp.transpose(measured, (1, 0, 2)),
        ((0, 0), (0, 0), (z.left, z.width_p - z.left - z.band)),
    )
    segment_lanes = up_to(3 * z.layers * z.tap_lanes, LANES)
    angle_value = 2.0 * math.pi / N_VIEWS * angle_index.astype(jnp.float32)
    sine = jnp.broadcast_to(jnp.sin(angle_value)[:, None], (z.angles, segment_lanes))
    slice_at = (
        jnp.arange(z.depth, dtype=jnp.int32)[:, None] * z.slices
        + jnp.arange(segment_lanes, dtype=jnp.int32)[None, :] % z.slices
    )
    cosine = jnp.cos(math.pi / z.total_slices * (slice_at.astype(jnp.float32) + 0.5))[:, None, :]

    message = call(pack_kernel, z, (z.depth, z.rows, z.message), [SMEM, VMEM, VMEM])(
        place, volume.reshape(z.rows, z.columns), extra
    )
    message = lax.all_to_all(message, "depth", 0, 0)
    partial = call(
        project_kernel,
        z,
        (z.layers + 1, z.angles, z.width_p),
        [SMEM, SMEM, VMEM, VMEM, VMEM, VMEM],
        [pltpu.VMEM((z.width_p // LANES * z.angles * SUB, LANES), jnp.float32)],
    )(place, band_offset, message, own, sine, cosine)
    below = shifted(partial[z.layers], "height", 1)
    above = shifted(partial[0], "height", -1)
    weight = call(
        adjoint_kernel,
        z,
        (z.depth, z.layers * z.tap_lanes, 3 * z.angles * SUB),
        [VMEM, VMEM, VMEM],
        dtype=jnp.bfloat16,
    )(message, sine, cosine)
    field = call(
        backproject_kernel,
        z,
        (z.layers, z.depth, z.slices, z.field_p),
        [SMEM, SMEM, VMEM, VMEM, VMEM, VMEM, VMEM],
        [pltpu.VMEM((z.width_p // LANES * z.angles * SUB, LANES), jnp.float32)],
    )(place, band_offset, partial, below, above, message, weight)
    field = field.reshape(z.layers, z.total_slices, z.field_p)
    field_below = shifted(field, "height", 1)
    field_above = shifted(field, "height", -1)
    bands = call(
        denoise_kernel,
        z,
        (z.depth, z.layers, z.slices, z.band),
        [SMEM, VMEM, VMEM, VMEM],
    )(place, field_below, field, field_above)
    bands = lax.all_to_all(bands, "depth", 0, 0)
    return jnp.transpose(bands, (1, 2, 0, 3)).reshape(volume.shape)


def solution(mesh):
    in_specs = (
        P("height", "depth", None),
        P(None, "height", "depth"),
        P(None, None, "depth"),
        P(),
        P(),
    )
    out_specs = P("height", "depth", None)
    return jax.shard_map(
        per_device, mesh=mesh, in_specs=in_specs, out_specs=out_specs, check_vma=False
    )
```

time: 153 us -> 70.7 us (0.46)
  the two profiles are of different devices: /device:TPU:1 before, /device:TPU:2 now
where the time goes in v1:
time: 70.7 us; the launch traced here: 70 us
  Pallas kernels  19.6 us (28%)
  starting transfers between devices  15.3 us (22%)
  waiting for transfers between devices  14 us (20%)
  blocking collectives  11 us (16%)
  local copies, waits for them, and re-layouts  7.68 us (11%)
  other arithmetic  2.3 us (3%)
    all_to_all x1, blocking collectives, per_device(): bands = lax.all_to_all(bands, 'depth', 0, 0)  11 us
    ppermute x4, starting transfers between devices, shifted(): return lax.ppermute(value, axis, pairs)  9.38 us
    all_to_all x1, waiting for transfers between devices, per_device(): message = lax.all_to_all(message, 'depth', 0, 0)  8.68 us
    pallas_call x1, Pallas kernels, per_device(): call(project_kernel, z, (z.layers + 1, z.angles, z.width_p), [SMEM, SMEM,...  6.05 us
    all_to_all x1, starting transfers between devices, per_device(): message = lax.all_to_all(message, 'depth', 0, 0)  5.97 us
    ppermute x4, waiting for transfers between devices, shifted(): return lax.ppermute(value, axis, pairs)  5.27 us
    pallas_call x1, Pallas kernels, per_device(): call(backproject_kernel, z, (z.layers, z.depth, z.slices, z.field_p), [SM...  5 us
    unnamed x18, local copies, waits for them, and re-layouts  4.62 us
  transfers between devices with their start and end apart: 5, of which 3 were waited for; matrix products, arithmetic and copies ran while one was open for 3% of the time, Pallas kernels for 6%

profile of v1, /device:TPU:2, one launch (start us, length us, event | category | flops | bytes accessed | tf_op | source)
XLA Modules:
  0.0 70.0 jit_solution(16241979773624817590)
XLA Ops:
  0.0 0.8 %copy.40 = f32[16,2,256]{2,0,1:T(8,128)S(1)} copy(f32[16,2,256]{2,1,0:T(2,128)} %param.6) | data formatting | bytes 65536 | tf_op args[1]
  0.8 0.6 copy-done.5
  2.9 1.8 %pack_kernel.1 = f32[8,16,768]{2,1,0:T(8,128)} custom-call(s32[2]{0:T(128)} %pad_add_fusion.refs_0_, f32[16,2048]{1,0:T(8,128)} %bitcast.36, f32[3,16,256]{2,1,0:T(8,128)} %pad_maximum_fusion.refs_2_), custom_call_target="tpu_custom_call" | custom-call | tf_op jit(solution)/shard_map/pack_kernel/pallas_call | solution.py:372
  4.7 6.0 %all-to-all-start = ((f32[8,16,768]{2,1,0:T(8,128)}), f32[8,16,768]{2,1,0:T(8,128)S(1)}, u32[]{:S(2)}, u32[]{:S(2)}) async-start(f32[8,16,768]{2,1,0:T(8,128)} %pack_kernel.1), calls=%async_computation | async-start | bytes 786432 | tf_op jit(solution)/shard_map/all_to_all | solution.py:375
  10.7 0.7 copy.35.refs_1_
  11.3 0.7 %pad.32.refs_3_ = f32[2,16,512]{2,1,0:T(8,128)} pad(f32[2,16,256]{2,1,0:T(8,128)S(1)} %bitcast.35, f32[]{:T(128)} %constant.30.clone.1), padding=0_0x0_0x66_190 | pad | bytes 98308 | tf_op jit(solution)/shard_map/jit(_pad)/pad | solution.py:359
  12.1 0.6 copy-done.7
  12.7 0.9 %multiply_cosine_fusion.refs_5_.refs_2_ = f32[8,1,256]{2,1,0:T(1,128)} fusion(s32[256]{0:T(256)S(1)} %and_select_fusion, s32[8]{0:T(128)S(1)} %iota_multiply_fusion), kind=kLoop, calls=%fused_computation.20 | loop fusion | flops 8192 | bytes 9248 | tf_op jit(solution)/shard_map/cos | solution.py:370
  13.7 8.7 %all-to-all-done.refs_2_.refs_0_.refs_5_ = f32[8,16,768]{2,1,0:T(8,128)S(1)} async-done(((f32[8,16,768]{2,1,0:T(8,128)}), f32[8,16,768]{2,1,0:T(8,128)S(1)}, u32[]{:S(2)}, u32[]{:S(2)}) %all-to-all-start) | async-done | bytes 393248 | tf_op jit(solution)/shard_map/all_to_all | solution.py:375
  22.3 0.8 %broadcast_in_dim.2.refs_4_.refs_1_ = f32[16,256]{1,0:T(8,128)} broadcast(f32[16]{0:T(128)S(1)} %multiply_sine_fusion), dimensions={0} | broadcast | bytes 16448 | tf_op jit(solution)/shard_map/broadcast_in_dim | solution.py:365
  23.1 6.1 %project_kernel.1.refs_2_ = f32[3,16,512]{2,1,0:T(8,128)} custom-call(s32[2]{0:T(128)} %pad_add_fusion.refs_0_, s32[16,8]{1,0:T(8,128)} %copy.35.refs_1_, f32[8,16,768]{2,1,0:T(8,128)} %copy-done, f32[2,16,512]{2,1,0:T(8,128)} %pad.32.refs_3_, f32[16,256]{1,0:T(8,128)} %broadcast_in_dim.2.refs_4_.refs_1_, f32[8,1,256]{2,1,0:T(1,128)} %multiply_cosine_fusion.refs_5_.refs_2_), custom_call_target="tpu_custom_call" | custom-call | tf_op jit(solution)/shard_map/project_kernel/pallas_call | solution.py:376
  29.2 0.8 %slice_bitcast_fusion = (f32[16,512]{1,0:T(8,128)S(1)}, f32[16,512]{1,0:T(8,128)S(1)}) fusion(f32[3,16,512]{2,1,0:T(8,128)} %project_kernel.1.refs_2_), kind=kLoop, calls=%fused_computation.1 | loop fusion | bytes 131072 | tf_op jit(solution)/shard_map/squeeze | solution.py:384
  29.9 1.9 %collective-permute-start.1 = (f32[16,512]{1,0:T(8,128)S(1)}, f32[16,512]{1,0:T(8,128)S(1)}, u32[]{:S(2)}, u32[]{:S(2)}) collective-permute-start(f32[16,512]{1,0:T(8,128)S(1)} %get-tuple-element.5), channel_id=1, source_target_pairs={{1,0},{2,1},{3,2},{5,4},{6,5},{7,6},{9,8},{10,9},{11,10},{13,12},{... | collective-permute-start | bytes 98312 | tf_op jit(solution)/shard_map/ppermute | solution.py:327
  31.9 2.4 %collective-permute-start = (f32[16,512]{1,0:T(8,128)S(1)}, f32[16,512]{1,0:T(8,128)S(1)}, u32[]{:S(2)}, u32[]{:S(2)}) collective-permute-start(f32[16,512]{1,0:T(8,128)S(1)} %get-tuple-element.6), channel_id=1, source_target_pairs={{0,1},{1,2},{2,3},{4,5},{5,6},{6,7},{8,9},{9,10},{10,11},{12,13},{... | collective-permute-start | bytes 98312 | tf_op jit(solution)/shard_map/ppermute | solution.py:327
  34.3 4.1 %adjoint_kernel.1.refs_6_ = bf16[8,64,384]{2,1,0:T(8,128)(2,1)} custom-call(f32[8,16,768]{2,1,0:T(8,128)} %copy-done, f32[16,256]{1,0:T(8,128)} %broadcast_in_dim.2.refs_4_.refs_1_, f32[8,1,256]{2,1,0:T(1,128)} %multiply_cosine_fusion.refs_5_.refs_2_), custom_call_target="tpu_custom_call" | custom-call | tf_op jit(solution)/shard_map/adjoint_kernel/pallas_call | solution.py:385
  39.6 5.0 %backproject_kernel.1 = f32[2,8,8,384]{3,2,1,0:T(8,128)} custom-call(s32[2]{0:T(128)} %pad_add_fusion.refs_0_, s32[16,8]{1,0:T(8,128)} %copy.35.refs_1_, f32[3,16,512]{2,1,0:T(8,128)} %project_kernel.1.refs_2_, f32[16,512]{1,0:T(8,128)} %copy-done.4, f32[16,512]{1,0:T(8,128)} %copy-done.3, f32[8,16,768]{2,1,0:T(8,128)} %copy-done, ...), custom_call_target="tpu_custom_call" | custom-call | tf_op jit(solution)/shard_map/backproject_kernel/pallas_call | solution.py:392
  44.6 3.1 %collective-permute-start.3 = (f32[2,64,384]{2,1,0:T(8,128)}, f32[2,64,384]{2,1,0:T(8,128)S(1)}, u32[]{:S(2)}, u32[]{:S(2)}) collective-permute-start(f32[2,64,384]{2,1,0:T(8,128)} %bitcast.31), channel_id=1, source_target_pairs={{1,0},{2,1},{3,2},{5,4},{6,5},{7,6},{9,8},{10,9},{11,10},{13,12},{... | collective-permute-start | bytes 589832 | tf_op jit(solution)/shard_map/ppermute | solution.py:327
  47.8 1.9 %collective-permute-start.2 = (f32[2,64,384]{2,1,0:T(8,128)}, f32[2,64,384]{2,1,0:T(8,128)S(1)}, u32[]{:S(2)}, u32[]{:S(2)}) collective-permute-start(f32[2,64,384]{2,1,0:T(8,128)} %bitcast.32), channel_id=1, source_target_pairs={{0,1},{1,2},{2,3},{4,5},{5,6},{6,7},{8,9},{9,10},{10,11},{12,13},{... | collective-permute-start | bytes 589832 | tf_op jit(solution)/shard_map/ppermute | solution.py:327
  49.7 1.6 %collective-permute-done.3.refs_3_ = f32[2,64,384]{2,1,0:T(8,128)S(1)} collective-permute-done((f32[2,64,384]{2,1,0:T(8,128)}, f32[2,64,384]{2,1,0:T(8,128)S(1)}, u32[]{:S(2)}, u32[]{:S(2)}) %collective-permute-start.3) | collective-permute-done | bytes 196640 | tf_op jit(solution)/shard_map/ppermute | solution.py:327
  51.2 3.7 %collective-permute-done.2.refs_1_ = f32[2,64,384]{2,1,0:T(8,128)S(1)} collective-permute-done((f32[2,64,384]{2,1,0:T(8,128)}, f32[2,64,384]{2,1,0:T(8,128)S(1)}, u32[]{:S(2)}, u32[]{:S(2)}) %collective-permute-start.2) | collective-permute-done | bytes 196640 | tf_op jit(solution)/shard_map/ppermute | solution.py:327
  55.0 0.7 copy-done.2
  55.6 2.7 %denoise_kernel.1 = f32[8,2,8,256]{3,2,1,0:T(8,128)} custom-call(s32[2]{0:T(128)} %pad_add_fusion.refs_0_, f32[2,64,384]{2,1,0:T(8,128)} %copy-done.2, f32[2,64,384]{2,1,0:T(8,128)} %bitcast.33, f32[2,64,384]{2,1,0:T(8,128)} %copy-done.1), custom_call_target="tpu_custom_call" | custom-call | tf_op jit(solution)/shard_map/denoise_kernel/pallas_call | solution.py:402
  58.3 11.0 %all_to_all.10 = f32[8,2,8,256]{3,2,1,0:T(8,128)S(1)} all-to-all(f32[8,2,8,256]{3,2,1,0:T(8,128)} %denoise_kernel.1), channel_id=1, replica_groups=mesh['depth'=8,'height'=4] {'depth'}, dimensions={0} | all-to-all | bytes 262144 | tf_op jit(solution)/shard_map/all_to_all | solution.py:408
  69.3 0.7 copy.37
  (29 shorter events, 2.8 us)
Async XLA Ops:
  0.8 0.7 %copy-start.5 = (f32[4,16,8]{1,2,0:T(8,128)S(1)}, f32[4,16,8]{1,2,0:T(8,128)}, u32[]{:S(2)}) copy-start(f32[4,16,8]{1,2,0:T(8,128)} %param.7) | copy-start | bytes 6148
  4.7 6.0 %copy-start.6 = (s32[16,8]{0,1:T(8,128)S(1)}, s32[16,8]{0,1:T(8,128)}, u32[]{:S(2)}) copy-start(s32[16,8]{0,1:T(8,128)} %param.8) | copy-start | bytes 1540
  4.7 17.6 %all-to-all-start = ((f32[8,16,768]{2,1,0:T(8,128)}), f32[8,16,768]{2,1,0:T(8,128)S(1)}, u32[]{:S(2)}, u32[]{:S(2)}) async-start(f32[8,16,768]{2,1,0:T(8,128)} %pack_kernel.1), calls=%async_computation | async-start | bytes 786432 | tf_op jit(solution)/shard_map/all_to_all | solution.py:375
  12.0 0.7 copy-start.7
  22.3 0.8 %copy-start = (f32[8,16,768]{2,1,0:T(8,128)}, f32[8,16,768]{2,1,0:T(8,128)S(1)}, u32[]{:S(2)}) copy-start(f32[8,16,768]{2,1,0:T(8,128)S(1)} %all-to-all-done.refs_2_.refs_0_.refs_5_) | copy-start | bytes 1179652
  29.9 8.5 %collective-permute-start.1 = (f32[16,512]{1,0:T(8,128)S(1)}, f32[16,512]{1,0:T(8,128)S(1)}, u32[]{:S(2)}, u32[]{:S(2)}) collective-permute-start(f32[16,512]{1,0:T(8,128)S(1)} %get-tuple-element.5), channel_id=1, source_target_pairs={{1,0},{2,1},{3,2},{5,4},{6,5},{7,6},{9,8},{10,9},{11,10},{13,12},{... | collective-permute-start | bytes 98312 | tf_op jit(solution)/shard_map/ppermute | solution.py:327
  31.9 6.6 %collective-permute-start = (f32[16,512]{1,0:T(8,128)S(1)}, f32[16,512]{1,0:T(8,128)S(1)}, u32[]{:S(2)}, u32[]{:S(2)}) collective-permute-start(f32[16,512]{1,0:T(8,128)S(1)} %get-tuple-element.6), channel_id=1, source_target_pairs={{0,1},{1,2},{2,3},{4,5},{5,6},{6,7},{8,9},{9,10},{10,11},{12,13},{... | collective-permute-start | bytes 98312 | tf_op jit(solution)/shard_map/ppermute | solution.py:327
  38.4 0.6 copy-start.3
  39.0 0.6 copy-start.4
  44.6 6.6 %collective-permute-start.3 = (f32[2,64,384]{2,1,0:T(8,128)}, f32[2,64,384]{2,1,0:T(8,128)S(1)}, u32[]{:S(2)}, u32[]{:S(2)}) collective-permute-start(f32[2,64,384]{2,1,0:T(8,128)} %bitcast.31), channel_id=1, source_target_pairs={{1,0},{2,1},{3,2},{5,4},{6,5},{7,6},{9,8},{10,9},{11,10},{13,12},{... | collective-permute-start | bytes 589832 | tf_op jit(solution)/shard_map/ppermute | solution.py:327
  47.8 7.2 %collective-permute-start.2 = (f32[2,64,384]{2,1,0:T(8,128)}, f32[2,64,384]{2,1,0:T(8,128)S(1)}, u32[]{:S(2)}, u32[]{:S(2)}) collective-permute-start(f32[2,64,384]{2,1,0:T(8,128)} %bitcast.32), channel_id=1, source_target_pairs={{0,1},{1,2},{2,3},{4,5},{5,6},{6,7},{8,9},{9,10},{10,11},{12,13},{... | collective-permute-start | bytes 589832 | tf_op jit(solution)/shard_map/ppermute | solution.py:327
  51.2 3.7 %copy-start.1 = (f32[2,64,384]{2,1,0:T(8,128)}, f32[2,64,384]{2,1,0:T(8,128)S(1)}, u32[]{:S(2)}) copy-start(f32[2,64,384]{2,1,0:T(8,128)S(1)} %collective-permute-done.3.refs_3_) | copy-start | bytes 589828
  55.0 0.7 copy-start.2

commit v2 on v1

--- a/solution.py
+++ b/solution.py
@@ -7,6 +7,7 @@
 from jax.experimental.pallas import tpu as pltpu
 from jax.sharding import PartitionSpec as P
 
+
 OFFMAX = 64
 N_VIEWS = 720
 SWEEPS = 2
@@ -26,7 +27,7 @@
 
 
 class Sizes:
-    def __init__(self, volume, measured, taps, depth_count, height_count):
+    def __init__(self, volume, taps, depth_count, height_count):
         self.depth, self.height = depth_count, height_count
         self.layers, self.slices, self.columns = volume.shape
         self.taps, self.angles = taps.shape[:2]
@@ -46,18 +47,14 @@
             last = min(self.band, self.width + away * self.band - self.left)
             if last > first:
                 self.pieces.append((away, first, last))
-        self.reach = max(abs(piece[0]) for piece in self.pieces)
         self.piece_p = max(
             [last - first for away, first, last in self.pieces if away != 0] + [1]
         )
         self.tap_lanes = self.taps * self.slices
         self.aligned = self.vol_width // LANES * LANES
         self.tap_at = self.vol_width - self.aligned
-        self.piece_at = self.tap_at + self.tap_lanes
-        self.message = up_to(
-            self.vol_width + self.tap_lanes + self.layers * self.piece_p, LANES
-        )
-        self.extra = self.message - self.aligned
+        self.message = up_to(self.vol_width + self.tap_lanes, LANES)
+        self.piece_p = up_to(self.piece_p, LANES)
         self.rows = self.layers * self.slices
 
 
@@ -71,14 +68,38 @@
     return value if amount == 0 else pltpu.roll(value, width - amount, value.ndim - 1)
 
 
+def shift_tiles(tiles, amount, count):
+    turned = pltpu.roll(jnp.concatenate(tiles, axis=0), (LANES - amount) % LANES, 1)
+    keep = lane_index((SUB, LANES)) < LANES - amount
+    return [
+        jnp.where(keep, turned[i * SUB : (i + 1) * SUB], turned[(i + 1) * SUB : (i + 2) * SUB])
+        for i in range(count)
+    ]
+
+
+def for_bricks(z, step):
+    unroll = next(u for u in (8, 4, 2, 1) if z.depth % u == 0)
+    if unroll == z.depth:
+        for brick in range(z.depth):
+            step(brick)
+        return
+
+    def several(start, carry):
+        for inner in range(unroll):
+            step(start * unroll + inner)
+        return carry
+
+    lax.fori_loop(0, z.depth // unroll, several, 0)
+
+
 def split(value):
     high = value.astype(jnp.bfloat16).astype(jnp.float32)
     return high, value - high
 
 
-def pack_kernel(z, me_ref, volume_ref, extra_ref, out_ref):
+def pack_kernel(z, volume_ref, taps_ref, out_ref):
     front = up_to(z.vol_left, LANES)
-    back = up_to(z.vol_p + LANES, LANES)
+    back = up_to(z.message + LANES, LANES)
     padded = jnp.concatenate(
         [
             jnp.zeros((z.rows, front), jnp.float32),
@@ -87,9 +108,20 @@
         ],
         axis=1,
     )
-    me = me_ref[0]
+    block = jnp.concatenate(
+        [taps_ref[...], jnp.zeros((z.tap_lanes, LANES - z.angles), jnp.float32)], axis=1
+    )
+    block = jnp.concatenate(
+        [block, jnp.zeros((LANES - z.tap_lanes, LANES), jnp.float32)], axis=0
+    )
+    block = block.T[: z.rows]
+    block = jnp.concatenate(
+        [block, jnp.zeros((z.rows, z.message - z.aligned - LANES + LANES), jnp.float32)], axis=1
+    )
+    tail_width = z.message - z.aligned
+    block = roll_left(block, -z.tap_at)[:, :tail_width]
+    keep = lane_index((z.rows, tail_width)) < z.tap_at
     rolled = {}
-    lane = lane_index((z.rows, LANES))
     for target in range(z.depth):
         start = front + target * z.band - z.vol_left
         shift = start % LANES
@@ -97,14 +129,8 @@
             rolled[shift] = roll_left(padded, shift)
         begin = start - shift
         out_ref[target, :, : z.aligned] = rolled[shift][:, begin : begin + z.aligned]
-        away = jnp.clip(target - me, -z.reach, z.reach) + z.reach
-        extra = extra_ref[away]
-        tail = rolled[shift][:, begin + z.aligned : begin + z.aligned + LANES]
-        out_ref[target, :, z.aligned : z.aligned + LANES] = jnp.where(
-            lane < z.tap_at, tail, extra[:, :LANES]
-        )
-        if z.extra > LANES:
-            out_ref[target, :, z.aligned + LANES :] = extra[:, LANES:]
+        tail = rolled[shift][:, begin + z.aligned : begin + z.message]
+        out_ref[target, :, z.aligned :] = jnp.where(keep, tail, block)
 
 
 def tap_rows(z, message_ref, brick):
@@ -132,13 +158,15 @@
     return jnp.concatenate(blocks, axis=0)
 
 
-def project_kernel(z, me_ref, offset_ref, message_ref, own_ref, sine_ref, cosine_ref, out_ref, sum_ref):
+def project_kernel(z, me_ref, offset_ref, message_ref, own_ref, sine_ref, cosine_ref, *refs):
+    *piece_refs, out_ref, sum_ref = refs
     me = me_ref[0]
     inner = z.layers * z.tap_lanes
     segment_lanes = up_to(3 * inner, LANES)
     sum_ref[...] = jnp.zeros_like(sum_ref)
-
-    def brick_step(brick, carry):
+    count = z.width_p // LANES
+
+    def brick_step(brick):
         taps = tap_rows(z, message_ref, brick)
         taps = jnp.concatenate([taps] * (segment_lanes // LANES), axis=1)
         rise = 0.5 + 0.45 * sine_ref[...] * cosine_ref[brick]
@@ -153,8 +181,8 @@
             block = message_ref[brick, layer * z.slices : (layer + 1) * z.slices, : z.vol_p]
             high, low = split(block)
             for tap in range(z.taps):
-                highs.append(pltpu.roll(high, tap, 1) if tap else high)
-                lows.append(pltpu.roll(low, tap, 1) if tap else low)
+                highs.append(roll_left(high, z.taps - 1 - tap))
+                lows.append(roll_left(low, z.taps - 1 - tap))
         high = jnp.concatenate(highs, axis=0).astype(jnp.bfloat16)
         low = jnp.concatenate(lows, axis=0).astype(jnp.bfloat16)
         product = jnp.dot(
@@ -163,14 +191,16 @@
             preferred_element_type=jnp.float32,
         )
         for angle in range(z.angles):
-            amount = z.vol_p - (OFFMAX + z.taps - 1) + offset_ref[angle, brick]
-            moved = pltpu.roll(product[angle * SUB : (angle + 1) * SUB], amount, 1)
-            for tile in range(z.width_p // LANES):
+            tiles = [
+                product[angle * SUB : (angle + 1) * SUB, tile * LANES : (tile + 1) * LANES]
+                for tile in range(count + 1)
+            ]
+            moved = shift_tiles(tiles, OFFMAX - offset_ref[angle, brick], count)
+            for tile in range(count):
                 rows = pl.ds((tile * z.angles + angle) * SUB, SUB)
-                sum_ref[rows, :] = sum_ref[rows, :] + moved[:, tile * LANES : (tile + 1) * LANES]
-        return carry
-
-    lax.fori_loop(0, z.depth, brick_step, 0)
+                sum_ref[rows, :] = sum_ref[rows, :] + moved[tile]
+
+    for_bricks(z, brick_step)
     lane = lane_index((z.angles, z.width_p))
     column = me * z.band - z.left + lane
     inside = (column >= 0) & (column < z.columns)
@@ -184,19 +214,17 @@
         )
         if row < z.layers:
             window = own_ref[row]
+            order = 0
             for away, first, last in z.pieces:
                 if away == 0:
                     continue
-                source = jnp.clip(me - away, 0, z.depth - 1)
-                tail = message_ref[source, : z.angles, z.aligned :]
-                if z.extra < z.width_p:
-                    tail = jnp.concatenate(
-                        [tail, jnp.zeros((z.angles, z.width_p - z.extra), jnp.float32)], axis=1
-                    )
-                else:
-                    tail = tail[:, : z.width_p]
+                tail = piece_refs[order][row * z.angles : (row + 1) * z.angles]
+                order += 1
+                tail = jnp.concatenate(
+                    [tail, jnp.zeros((z.angles, z.width_p - z.piece_p), jnp.float32)], axis=1
+                )
                 begin = first - away * z.band + z.left
-                tail = roll_left(tail, z.piece_at + row * z.piece_p - begin)
+                tail = roll_left(tail, -begin)
                 here = (lane >= begin) & (lane < begin + last - first)
                 window = jnp.where(here, tail, window)
             total = total + window
@@ -206,45 +234,45 @@
 def adjoint_kernel(z, message_ref, sine_ref, cosine_ref, out_ref):
     inner = z.layers * z.tap_lanes
 
-    def brick_step(brick, carry):
+    def brick_step(brick):
         taps = tap_rows(z, message_ref, brick)
         rise = 0.5 + 0.45 * sine_ref[:, :LANES] * cosine_ref[brick, :, :LANES]
         spread = spread_rows(z, taps * (1.0 - rise), taps * rise)
         high, low = split(spread.T[:inner])
         out_ref[brick] = jnp.concatenate([high, low, high], axis=1).astype(jnp.bfloat16)
-        return carry
-
-    lax.fori_loop(0, z.depth, brick_step, 0)
-
-
-def backproject_kernel(z, place_ref, offset_ref, own_ref, below_ref, above_ref, message_ref, weight_ref, out_ref, row_ref):
+
+    for_bricks(z, brick_step)
+
+
+def backproject_kernel(z, place_ref, offset_ref, own_ref, near_ref, far_ref, message_ref, weight_ref, out_ref, row_ref):
     row_ref[...] = jnp.zeros_like(row_ref)
     last = place_ref[1] == z.height - 1
+    even = place_ref[1] % 2 == 0
+    below = jnp.where(even, far_ref[...], near_ref[...])
+    above = jnp.where(even, near_ref[...], far_ref[...])
     for row in range(z.layers + 1):
         value = own_ref[row]
         if row == 0:
-            value = value + below_ref[...]
+            value = value + below
         if row == z.layers:
-            value = jnp.where(last, 0.0, value + above_ref[...])
+            value = jnp.where(last, 0.0, value + above)
         for tile in range(z.width_p // LANES):
             row_ref[pl.ds(tile * z.angles * SUB + row, z.angles, SUB), :] = value[
                 :, tile * LANES : (tile + 1) * LANES
             ]
     lead = z.vol_left - SWEEPS
 
-    def brick_step(brick, carry):
+    count = z.field_p // LANES
+
+    def brick_step(brick):
         blocks = []
         for angle in range(z.angles):
-            amount = (z.width_p - OFFMAX - offset_ref[angle, brick]) % z.width_p
-            block = jnp.concatenate(
-                [
-                    row_ref[pl.ds((tile * z.angles + angle) * SUB, SUB), :]
-                    for tile in range(z.width_p // LANES)
-                ],
-                axis=1,
-            )
-            block = pltpu.roll(block, amount, 1)
-            blocks.append(block[:, : z.field_p])
+            tiles = [
+                row_ref[pl.ds((tile * z.angles + angle) * SUB, SUB), :]
+                for tile in range(count + 1)
+            ]
+            moved = shift_tiles(tiles, OFFMAX + offset_ref[angle, brick], count)
+            blocks.append(jnp.concatenate(moved, axis=1))
         high, low = split(jnp.concatenate(blocks, axis=0))
         high = high.astype(jnp.bfloat16)
         low = low.astype(jnp.bfloat16)
@@ -265,12 +293,11 @@
             ]
             voxels = roll_left(voxels, lead - start)[:, : z.field_p]
             out_ref[layer, brick] = voxels + relax_step * update
-        return carry
-
-    lax.fori_loop(0, z.depth, brick_step, 0)
-
-
-def denoise_kernel(z, place_ref, below_ref, own_ref, above_ref, out_ref):
+
+    for_bricks(z, brick_step)
+
+
+def denoise_kernel(z, place_ref, near_ref, own_ref, far_ref, out_ref):
     shape = (z.total_slices, z.field_p)
     column = place_ref[0] * z.band - SWEEPS + lane_index(shape)
     slice_at = lax.broadcasted_iota(jnp.int32, shape, 0)
@@ -278,14 +305,19 @@
     allow_y = slice_at + 1 < z.total_slices
     not_first = slice_at > 0
     first_layer = place_ref[1] * z.layers
+    even = place_ref[1] % 2 == 0
     values = {}
     for layer in range(-SWEEPS, z.layers + SWEEPS):
         if layer < 0:
-            values[layer] = below_ref[z.layers + layer]
+            values[layer] = jnp.where(
+                even, far_ref[z.layers + layer], near_ref[z.layers + layer]
+            )
         elif layer < z.layers:
             values[layer] = own_ref[layer]
         else:
-            values[layer] = above_ref[layer - z.layers]
+            values[layer] = jnp.where(
+                even, near_ref[layer - z.layers], far_ref[layer - z.layers]
+            )
     for sweep in range(SWEEPS):
         margin = SWEEPS - 1 - sweep
         later = {}
@@ -327,35 +359,39 @@
     return lax.ppermute(value, axis, pairs)
 
 
-def call(kernel, z, shape, specs, scratch=(), dtype=jnp.float32, cycles=2000):
+def swapped(value, axis, first):
+    count = lax.axis_size(axis)
+    pairs = []
+    for low in range(first, count - 1, 2):
+        pairs += [(low, low + 1), (low + 1, low)]
+    return lax.ppermute(value, axis, pairs)
+
+
+def call(kernel, z, shape, specs, scratch=(), dtype=jnp.float32, limit=16 << 20):
     return pl.pallas_call(
         lambda *refs: kernel(z, *refs),
         out_shape=jax.ShapeDtypeStruct(shape, dtype),
         in_specs=specs,
         out_specs=VMEM,
         scratch_shapes=list(scratch),
-        name=kernel.__name__,
+        compiler_params=pltpu.CompilerParams(vmem_limit_bytes=limit),
     )
 
 
 def per_device(volume, measured, taps, band_offset, angle_index):
-    z = Sizes(volume, measured, taps, lax.axis_size("depth"), lax.axis_size("height"))
+    z = Sizes(volume, taps, lax.axis_size("depth"), lax.axis_size("height"))
     depth_of = lax.axis_index("depth")
     height_of = lax.axis_index("height")
     place = jnp.stack([depth_of, height_of]).astype(jnp.int32)
 
-    tap_part = jnp.transpose(taps, (1, 0, 2)).reshape(z.angles, z.tap_lanes)
-    extras = []
-    table = {away: (first, last) for away, first, last in z.pieces}
-    for away in range(-z.reach, z.reach + 1):
-        parts = [jnp.zeros((z.angles, z.tap_at), jnp.float32), tap_part]
-        for row in range(z.layers):
-            first, last = table[away] if away != 0 else (0, 0)
-            piece = measured[:, row, first:last]
-            parts.append(jnp.pad(piece, ((0, 0), (0, z.piece_p - (last - first)))))
-        joined = jnp.concatenate(parts, axis=1)
-        extras.append(jnp.pad(joined, ((0, z.rows - z.angles), (0, z.extra - joined.shape[1]))))
-    extra = jnp.stack(extras)
+    pieces = []
+    for away, first, last in z.pieces:
+        if away == 0:
+            continue
+        piece = jnp.transpose(measured[:, :, first:last], (1, 0, 2))
+        piece = jnp.pad(piece, ((0, 0), (0, 0), (0, z.piece_p - (last - first))))
+        piece = piece.reshape(z.layers * z.angles, z.piece_p)
+        pieces.append(shifted(piece, "depth", away))
     own = jnp.pad(
         jnp.transpose(measured, (1, 0, 2)),
         ((0, 0), (0, 0), (z.left, z.width_p - z.left - z.band)),
@@ -369,19 +405,24 @@
     )
     cosine = jnp.cos(math.pi / z.total_slices * (slice_at.astype(jnp.float32) + 0.5))[:, None, :]
 
-    message = call(pack_kernel, z, (z.depth, z.rows, z.message), [SMEM, VMEM, VMEM])(
-        place, volume.reshape(z.rows, z.columns), extra
+    message = call(
+        pack_kernel, z, (z.depth, z.rows, z.message), [VMEM, VMEM], limit=None
+    )(
+        volume.reshape(z.rows, z.columns),
+        jnp.transpose(taps, (0, 2, 1)).reshape(z.tap_lanes, z.angles),
     )
     message = lax.all_to_all(message, "depth", 0, 0)
     partial = call(
         project_kernel,
         z,
         (z.layers + 1, z.angles, z.width_p),
-        [SMEM, SMEM, VMEM, VMEM, VMEM, VMEM],
+        [SMEM, SMEM, VMEM, VMEM, VMEM, VMEM] + [VMEM] * len(pieces),
         [pltpu.VMEM((z.width_p // LANES * z.angles * SUB, LANES), jnp.float32)],
-    )(place, band_offset, message, own, sine, cosine)
-    below = shifted(partial[z.layers], "height", 1)
-    above = shifted(partial[0], "height", -1)
+    )(place, band_offset, message, own, sine, cosine, *pieces)
+    even = height_of % 2 == 0
+    upward, downward = partial[z.layers], partial[0]
+    far = swapped(jnp.where(even, downward, upward), "height", 1)
+    near = swapped(jnp.where(even, upward, downward), "height", 0)
     weight = call(
         adjoint_kernel,
         z,
@@ -395,16 +436,16 @@
         (z.layers, z.depth, z.slices, z.field_p),
         [SMEM, SMEM, VMEM, VMEM, VMEM, VMEM, VMEM],
         [pltpu.VMEM((z.width_p // LANES * z.angles * SUB, LANES), jnp.float32)],
-    )(place, band_offset, partial, below, above, message, weight)
+    )(place, band_offset, partial, near, far, message, weight)
     field = field.reshape(z.layers, z.total_slices, z.field_p)
-    field_below = shifted(field, "height", 1)
-    field_above = shifted(field, "height", -1)
+    field_far = swapped(field, "height", 1)
+    field_near = swapped(field, "height", 0)
     bands = call(
         denoise_kernel,
         z,
         (z.depth, z.layers, z.slices, z.band),
         [SMEM, VMEM, VMEM, VMEM],
-    )(place, field_below, field, field_above)
+    )(place, field_near, field, field_far)
     bands = lax.all_to_all(bands, "depth", 0, 0)
     return jnp.transpose(bands, (1, 2, 0, 3)).reshape(volume.shape)
 
@@ -418,6 +459,7 @@
         P(),
     )
     out_specs = P("height", "depth", None)
+
     return jax.shard_map(
         per_device, mesh=mesh, in_specs=in_specs, out_specs=out_specs, check_vma=False
     )

time: 70.7 us -> 54.6 us (0.77)
  the two profiles are of different devices: /device:TPU:2 before, /device:TPU:1 now
where the time goes in v2:
time: 54.6 us; the launch traced here: 53.7 us
  starting transfers between devices  21.8 us (40%)
  waiting for transfers between devices  10.2 us (19%)
  blocking collectives  9.44 us (17%)
  Pallas kernels  8.65 us (16%)
  local copies, waits for them, and re-layouts  3.04 us (6%)
    ppermute x4, starting transfers between devices, swapped(): return lax.ppermute(value, axis, pairs)  10.2 us
    all_to_all x1, blocking collectives, per_device(): bands = lax.all_to_all(bands, 'depth', 0, 0)  9.44 us
    ppermute x2, starting transfers between devices, shifted(): return lax.ppermute(value, axis, pairs)  5.88 us
    all_to_all x1, waiting for transfers between devices, per_device(): message = lax.all_to_all(message, 'depth', 0, 0)  5.81 us
    all_to_all x1, starting transfers between devices, per_device(): message = lax.all_to_all(message, 'depth', 0, 0)  5.66 us
    ppermute x4, waiting for transfers between devices, swapped(): return lax.ppermute(value, axis, pairs)  4.37 us
    pallas_call x1, Pallas kernels, per_device(): call(project_kernel, z, (z.layers + 1, z.angles, z.width_p), [SMEM, SMEM,...  2.97 us
    pallas_call x1, Pallas kernels, per_device(): call(backproject_kernel, z, (z.layers, z.depth, z.slices, z.field_p), [SM...  2.04 us
  transfers between devices with their start and end apart: 7, of which 3 were waited for; matrix products, arithmetic and copies ran while one was open for 1% of the time, Pallas kernels for 4%

profile of v2, /device:TPU:1, one launch (start us, length us, event | category | flops | bytes accessed | tf_op | source)
XLA Modules:
  0.0 53.7 jit_solution(4506436671070958601)
XLA Ops:
  0.0 0.7 %slice_bitcast_fusion.1 = f32[2,16,69]{2,0,1:T(2,128)S(1)} fusion(f32[16,2,256]{2,1,0:T(2,128)} %param.6), kind=kLoop, calls=%fused_computation.4 | loop fusion | bytes 17664 | tf_op jit(solution)/shard_map/transpose | solution.py:391
  0.7 1.3 %collective-permute-start = (f32[32,128]{1,0:T(8,128)S(1)}, f32[32,128]{1,0:T(8,128)S(1)}, u32[]{:S(2)}, u32[]{:S(2)}) collective-permute-start(f32[32,128]{1,0:T(8,128)S(1)} %bitcast.29), channel_id=1, source_target_pairs={{4,0},{8,4},{12,8},{16,12},{20,16},{24,20},{28,24},{5,1},{9,5},{13... | collective-permute-start | bytes 49160 | tf_op jit(solution)/shard_map/ppermute | solution.py:359
  2.0 0.1 slice_bitcast_fusion
  2.1 4.6 %collective-permute-start.1 = (f32[32,128]{1,0:T(8,128)S(1)}, f32[32,128]{1,0:T(8,128)S(1)}, u32[]{:S(2)}, u32[]{:S(2)}) collective-permute-start(f32[32,128]{1,0:T(8,128)S(1)} %bitcast.30), channel_id=1, source_target_pairs={{0,4},{4,8},{8,12},{12,16},{16,20},{20,24},{24,28},{1,5},{5,9},{9,... | collective-permute-start | bytes 49160 | tf_op jit(solution)/shard_map/ppermute | solution.py:359
  6.7 1.8 %shard_map.55 = f32[8,16,640]{2,1,0:T(8,128)} custom-call(f32[16,2048]{1,0:T(8,128)} %bitcast.28, f32[32,16]{1,0:T(8,128)} %bitcast.31), custom_call_target="tpu_custom_call" | custom-call | tf_op jit(solution)/shard_map/pallas_call | solution.py:408
  8.5 5.7 %all-to-all-start = ((f32[8,16,640]{2,1,0:T(8,128)}), f32[8,16,640]{2,1,0:T(8,128)S(1)}, u32[]{:S(2)}, u32[]{:S(2)}) async-start(f32[8,16,640]{2,1,0:T(8,128)} %shard_map.55), calls=%async_computation | async-start | bytes 655360 | tf_op jit(solution)/shard_map/all_to_all | solution.py:414
  14.2 0.6 %copy-done.2 = s32[16]{0:T(128)S(1)} copy-done((s32[16]{0:T(128)S(1)}, s32[16]{0:T(128)}, u32[]{:S(2)}) %copy-start.2) | copy-done | bytes 88
  14.9 0.3 multiply_cosine_fusion.refs_5_.refs_2_
  15.2 0.1 pad_add_fusion.refs_0_
  15.3 0.7 %copy-done.1 = s32[16,8]{0,1:T(8,128)S(1)} copy-done((s32[16,8]{0,1:T(8,128)S(1)}, s32[16,8]{0,1:T(8,128)}, u32[]{:S(2)}) %copy-start.1) | copy-done | bytes 536
  16.0 0.1 pad.12.refs_3_
  16.1 5.8 %all-to-all-done.refs_2_.refs_0_.refs_5_ = f32[8,16,640]{2,1,0:T(8,128)S(1)} async-done(((f32[8,16,640]{2,1,0:T(8,128)}), f32[8,16,640]{2,1,0:T(8,128)S(1)}, u32[]{:S(2)}, u32[]{:S(2)}) %all-to-all-start) | async-done | bytes 327712 | tf_op jit(solution)/shard_map/all_to_all | solution.py:414
  22.0 3.0 %shard_map.56.refs_2_ = f32[3,16,512]{2,1,0:T(8,128)S(1)} custom-call(s32[2]{0:T(128)S(1)} %pad_add_fusion.refs_0_, s32[16,8]{1,0:T(8,128)S(1)} %copy.22.refs_1_, f32[8,16,640]{2,1,0:T(8,128)S(1)} %all-to-all-done.refs_2_.refs_0_.refs_5_, f32[2,16,512]{2,1,0:T(8,128)S(1)} %pad.12.refs_3_, f32[16,256]{1,0:T(8,128)S(1)} %broadcast_in_dim.2.refs_4_.refs_1_, ...), custom_call_target="tpu_custom_call" | custom-call | tf_op jit(solution)/shard_map/pallas_call | solution.py:415
  25.0 6.5 %collective-permute-start.3 = (f32[16,512]{1,0:T(8,128)S(1)}, f32[16,512]{1,0:T(8,128)S(1)}, u32[]{:S(2)}, u32[]{:S(2)}) collective-permute-start(f32[16,512]{1,0:T(8,128)S(1)} %get-tuple-element.5), channel_id=1, source_target_pairs={{1,2},{2,1},{5,6},{6,5},{9,10},{10,9},{13,14},{14,13},{17,18},{18,... | collective-permute-start | bytes 98312 | tf_op jit(solution)/shard_map/ppermute | solution.py:367
  31.5 0.1 collective-permute-start.2
  31.6 0.4 shard_map.57.refs_6_
  32.0 1.1 %collective-permute-done.3.refs_4_ = f32[16,512]{1,0:T(8,128)S(1)} collective-permute-done((f32[16,512]{1,0:T(8,128)S(1)}, f32[16,512]{1,0:T(8,128)S(1)}, u32[]{:S(2)}, u32[]{:S(2)}) %collective-permute-start.3) | collective-permute-done | bytes 32800 | tf_op jit(solution)/shard_map/ppermute | solution.py:367
  33.1 2.0 %shard_map.58 = f32[2,8,8,384]{3,2,1,0:T(8,128)S(1)} custom-call(s32[2]{0:T(128)S(1)} %pad_add_fusion.refs_0_, s32[16,8]{1,0:T(8,128)S(1)} %copy.22.refs_1_, f32[3,16,512]{2,1,0:T(8,128)S(1)} %shard_map.56.refs_2_, f32[16,512]{1,0:T(8,128)S(1)} %collective-permute-done.2.refs_3_, f32[16,512]{1,0:T(8,128)S(1)} %collective-permute-done.3.refs_4_, ...), custom_call_target="tpu_custom_call" | custom-call | tf_op jit(solution)/shard_map/pallas_call | solution.py:433
  35.1 3.6 %collective-permute-start.5 = (f32[2,64,384]{2,1,0:T(8,128)S(1)}, f32[2,64,384]{2,1,0:T(8,128)S(1)}, u32[]{:S(2)}, u32[]{:S(2)}) collective-permute-start(f32[2,64,384]{2,1,0:T(8,128)S(1)} %bitcast.23), channel_id=1, source_target_pairs={{1,2},{2,1},{5,6},{6,5},{9,10},{10,9},{13,14},{14,13},{17,18},{18,... | collective-permute-start | bytes 589832 | tf_op jit(solution)/shard_map/ppermute | solution.py:367
  38.8 0.1 collective-permute-start.4
  38.9 3.3 %collective-permute-done.5.refs_3_ = f32[2,64,384]{2,1,0:T(8,128)S(1)} collective-permute-done((f32[2,64,384]{2,1,0:T(8,128)S(1)}, f32[2,64,384]{2,1,0:T(8,128)S(1)}, u32[]{:S(2)}, u32[]{:S(2)}) %collective-permute-start.5) | collective-permute-done | bytes 196640 | tf_op jit(solution)/shard_map/ppermute | solution.py:367
  42.1 1.5 %shard_map.59 = f32[8,2,8,256]{3,2,1,0:T(8,128)S(1)} custom-call(s32[2]{0:T(128)S(1)} %pad_add_fusion.refs_0_, f32[2,64,384]{2,1,0:T(8,128)S(1)} %collective-permute-done.4.refs_1_, f32[2,64,384]{2,1,0:T(8,128)S(1)} %bitcast.25, f32[2,64,384]{2,1,0:T(8,128)S(1)} %collective-permute-done.5.refs_3_), custom_call_target="tpu_custom_call" | custom-call | tf_op jit(solution)/shard_map/pallas_call | solution.py:443
  43.6 9.4 %all_to_all.10 = f32[8,2,8,256]{3,2,1,0:T(8,128)S(1)} all-to-all(f32[8,2,8,256]{3,2,1,0:T(8,128)S(1)} %shard_map.59), channel_id=1, replica_groups=mesh['depth'=8,'height'=4] {'depth'}, dimensions={0} | all-to-all | bytes 262144 | tf_op jit(solution)/shard_map/all_to_all | solution.py:449
  53.0 0.7 %copy.26 = f32[8,2,1,8,256]{4,3,0,2,1:T(8,128)} copy(f32[8,2,1,8,256]{4,3,2,1,0:T(8,128)S(1)} %bitcast.26) | data formatting | bytes 262144 | tf_op jit(solution)/shard_map/reshape | solution.py:450
  (19 shorter events, 0.2 us)
Async XLA Ops:
  0.7 1.3 %copy-start = (f32[16,2,256]{2,1,0:T(2,128)S(1)}, f32[16,2,256]{2,1,0:T(2,128)}, u32[]{:S(2)}) copy-start(f32[16,2,256]{2,1,0:T(2,128)} %param.6) | copy-start | bytes 98308
  0.7 15.4 %collective-permute-start = (f32[32,128]{1,0:T(8,128)S(1)}, f32[32,128]{1,0:T(8,128)S(1)}, u32[]{:S(2)}, u32[]{:S(2)}) collective-permute-start(f32[32,128]{1,0:T(8,128)S(1)} %bitcast.29), channel_id=1, source_target_pairs={{4,0},{8,4},{12,8},{16,12},{20,16},{24,20},{28,24},{5,1},{9,5},{13... | collective-permute-start | bytes 49160 | tf_op jit(solution)/shard_map/ppermute | solution.py:359
  2.1 14.0 %collective-permute-start.1 = (f32[32,128]{1,0:T(8,128)S(1)}, f32[32,128]{1,0:T(8,128)S(1)}, u32[]{:S(2)}, u32[]{:S(2)}) collective-permute-start(f32[32,128]{1,0:T(8,128)S(1)} %bitcast.30), channel_id=1, source_target_pairs={{0,4},{4,8},{8,12},{12,16},{16,20},{20,24},{24,28},{1,5},{5,9},{9,... | collective-permute-start | bytes 49160 | tf_op jit(solution)/shard_map/ppermute | solution.py:359
  8.5 13.4 %all-to-all-start = ((f32[8,16,640]{2,1,0:T(8,128)}), f32[8,16,640]{2,1,0:T(8,128)S(1)}, u32[]{:S(2)}, u32[]{:S(2)}) async-start(f32[8,16,640]{2,1,0:T(8,128)} %shard_map.55), calls=%async_computation | async-start | bytes 655360 | tf_op jit(solution)/shard_map/all_to_all | solution.py:414
  14.2 0.7 %copy-start.2 = (s32[16]{0:T(128)S(1)}, s32[16]{0:T(128)}, u32[]{:S(2)}) copy-start(s32[16]{0:T(128)} %param.9) | copy-start | bytes 196
  15.3 0.7 %copy-start.1 = (s32[16,8]{0,1:T(8,128)S(1)}, s32[16,8]{0,1:T(8,128)}, u32[]{:S(2)}) copy-start(s32[16,8]{0,1:T(8,128)} %param.8) | copy-start | bytes 1540
  25.0 8.1 %collective-permute-start.3 = (f32[16,512]{1,0:T(8,128)S(1)}, f32[16,512]{1,0:T(8,128)S(1)}, u32[]{:S(2)}, u32[]{:S(2)}) collective-permute-start(f32[16,512]{1,0:T(8,128)S(1)} %get-tuple-element.5), channel_id=1, source_target_pairs={{1,2},{2,1},{5,6},{6,5},{9,10},{10,9},{13,14},{14,13},{17,18},{18,... | collective-permute-start | bytes 98312 | tf_op jit(solution)/shard_map/ppermute | solution.py:367
  31.5 1.6 %collective-permute-start.2 = (f32[16,512]{1,0:T(8,128)S(1)}, f32[16,512]{1,0:T(8,128)S(1)}, u32[]{:S(2)}, u32[]{:S(2)}) collective-permute-start(f32[16,512]{1,0:T(8,128)S(1)} %get-tuple-element.6), channel_id=1, source_target_pairs={{0,1},{1,0},{2,3},{3,2},{4,5},{5,4},{6,7},{7,6},{8,9},{9,8},{10,11... | collective-permute-start | bytes 98312 | tf_op jit(solution)/shard_map/ppermute | solution.py:367
  35.1 7.0 %collective-permute-start.5 = (f32[2,64,384]{2,1,0:T(8,128)S(1)}, f32[2,64,384]{2,1,0:T(8,128)S(1)}, u32[]{:S(2)}, u32[]{:S(2)}) collective-permute-start(f32[2,64,384]{2,1,0:T(8,128)S(1)} %bitcast.23), channel_id=1, source_target_pairs={{1,2},{2,1},{5,6},{6,5},{9,10},{10,9},{13,14},{14,13},{17,18},{18,... | collective-permute-start | bytes 589832 | tf_op jit(solution)/shard_map/ppermute | solution.py:367
  38.8 3.3 %collective-permute-start.4 = (f32[2,64,384]{2,1,0:T(8,128)S(1)}, f32[2,64,384]{2,1,0:T(8,128)S(1)}, u32[]{:S(2)}, u32[]{:S(2)}) collective-permute-start(f32[2,64,384]{2,1,0:T(8,128)S(1)} %bitcast.24), channel_id=1, source_target_pairs={{0,1},{1,0},{2,3},{3,2},{4,5},{5,4},{6,7},{7,6},{8,9},{9,8},{10,11... | collective-permute-start | bytes 589832 | tf_op jit(solution)/shard_map/ppermute | solution.py:367

commit v3 on v2

--- a/solution.py
+++ b/solution.py
@@ -39,8 +39,14 @@
         self.vol_width = self.width + 2 * OFFMAX + self.taps - 1
         self.field = self.band + 2 * SWEEPS
         self.width_p = up_to(self.width, LANES)
-        self.vol_p = up_to(self.vol_width, LANES)
-        self.field_p = up_to(self.field + self.taps - 1, LANES)
+        self.lead = self.vol_left - SWEEPS
+        self.lag = self.lead % LANES
+        self.field_p = up_to(self.field + self.lag, LANES)
+        self.half = -(-self.width_p // LANES // 2)
+        self.margin = SWEEPS
+        self.near_layers = self.layers + 2 * self.margin
+        if self.layers != self.margin or self.lag != self.taps - 1:
+            raise ValueError("unsupported sizes")
         self.pieces = []
         for away in range(-depth_count + 1, depth_count):
             first = max(0, away * self.band - self.left)
@@ -54,6 +60,7 @@
         self.aligned = self.vol_width // LANES * LANES
         self.tap_at = self.vol_width - self.aligned
         self.message = up_to(self.vol_width + self.tap_lanes, LANES)
+        self.message = max(self.message, (2 * self.half + 1) * LANES)
         self.piece_p = up_to(self.piece_p, LANES)
         self.rows = self.layers * self.slices
 
@@ -69,7 +76,7 @@
 
 
 def shift_tiles(tiles, amount, count):
-    turned = pltpu.roll(jnp.concatenate(tiles, axis=0), (LANES - amount) % LANES, 1)
+    turned = pltpu.roll(jnp.concatenate(tiles, axis=0), (LANES - amount) & (LANES - 1), 1)
     keep = lane_index((SUB, LANES)) < LANES - amount
     return [
         jnp.where(keep, turned[i * SUB : (i + 1) * SUB], turned[(i + 1) * SUB : (i + 2) * SUB])
@@ -145,58 +152,71 @@
     return tile
 
 
-def spread_rows(z, low, high):
-    width = low.shape[1]
-    layer = lane_index((SUB, width)) % (z.layers * z.tap_lanes) // z.tap_lanes
-    row = lax.broadcasted_iota(jnp.int32, (SUB, width), 0)
-    same, above = row == layer, row == layer + 1
-    blocks = []
-    for angle in range(z.angles):
-        first = jnp.broadcast_to(low[angle : angle + 1], (SUB, width))
-        second = jnp.broadcast_to(high[angle : angle + 1], (SUB, width))
-        blocks.append(jnp.where(same, first, jnp.where(above, second, 0.0)))
-    return jnp.concatenate(blocks, axis=0)
+def row_masks(lane_layer, lane_segment):
+    row = lax.broadcasted_iota(jnp.int32, lane_layer.shape, 0)
+    inside = lane_segment == row // 4
+    return inside & (row % 4 == lane_layer), inside & (row % 4 == lane_layer + 1)
 
 
 def project_kernel(z, me_ref, offset_ref, message_ref, own_ref, sine_ref, cosine_ref, *refs):
-    *piece_refs, out_ref, sum_ref = refs
+    *piece_refs, out_ref, sum_ref, part_ref = refs
     me = me_ref[0]
     inner = z.layers * z.tap_lanes
-    segment_lanes = up_to(3 * inner, LANES)
+    tiles = 2 * 3 * inner // LANES
+    count = z.width_p // LANES
+    reach = (z.half + 1) * LANES
     sum_ref[...] = jnp.zeros_like(sum_ref)
-    count = z.width_p // LANES
+    masks, middles = [], []
+    for tile in range(tiles):
+        lane = tile * LANES + lane_index((SUB, LANES))
+        masks.append(row_masks(lane % inner // z.tap_lanes, lane // (3 * inner)))
+        lane = tile * LANES + lane_index((z.angles, LANES))
+        middles.append(lane // inner % 3 == 1)
 
     def brick_step(brick):
         taps = tap_rows(z, message_ref, brick)
-        taps = jnp.concatenate([taps] * (segment_lanes // LANES), axis=1)
         rise = 0.5 + 0.45 * sine_ref[...] * cosine_ref[brick]
-        middle = lane_index(taps.shape) // inner == 1
-        parts = []
-        for weight in (taps * (1.0 - rise), taps * rise):
+        for side, weight in enumerate((taps * (1.0 - rise), taps * rise)):
             high, low = split(weight)
-            parts.append(jnp.where(middle, low, high))
-        left = spread_rows(z, parts[0], parts[1])[:, : 3 * inner].astype(jnp.bfloat16)
+            for tile in range(tiles):
+                at = ((brick * 2 + side) * tiles + tile) * z.angles
+                part_ref[pl.ds(at, z.angles), :] = jnp.where(middles[tile], low, high)
+        blocks = []
+        for angle in range(z.angles):
+            row = []
+            for tile in range(tiles):
+                at = (brick * 2 * tiles + tile) * z.angles + angle
+                first = part_ref[pl.ds(at, SUB, 0), :]
+                second = part_ref[pl.ds(at + tiles * z.angles, SUB, 0), :]
+                same, above = masks[tile]
+                row.append(jnp.where(same, first, jnp.where(above, second, 0.0)))
+            blocks.append(jnp.concatenate(row, axis=1))
+        left = jnp.concatenate(blocks, axis=0).astype(jnp.bfloat16)
         highs, lows = [], []
         for layer in range(z.layers):
-            block = message_ref[brick, layer * z.slices : (layer + 1) * z.slices, : z.vol_p]
-            high, low = split(block)
+            block = message_ref[
+                brick, layer * z.slices : (layer + 1) * z.slices, : (2 * z.half + 1) * LANES
+            ]
             for tap in range(z.taps):
-                highs.append(roll_left(high, z.taps - 1 - tap))
-                lows.append(roll_left(low, z.taps - 1 - tap))
+                high, low = split(roll_left(block, z.taps - 1 - tap))
+                highs.append(high)
+                lows.append(low)
         high = jnp.concatenate(highs, axis=0).astype(jnp.bfloat16)
         low = jnp.concatenate(lows, axis=0).astype(jnp.bfloat16)
+        right = []
+        for begin in (0, z.half * LANES):
+            part = high[:, begin : begin + reach]
+            right += [part, part, low[:, begin : begin + reach]]
         product = jnp.dot(
-            left,
-            jnp.concatenate([high, high, low], axis=0),
-            preferred_element_type=jnp.float32,
+            left, jnp.concatenate(right, axis=0), preferred_element_type=jnp.float32
         )
         for angle in range(z.angles):
-            tiles = [
+            pieces = [
                 product[angle * SUB : (angle + 1) * SUB, tile * LANES : (tile + 1) * LANES]
-                for tile in range(count + 1)
+                for tile in range(z.half + 1)
             ]
-            moved = shift_tiles(tiles, OFFMAX - offset_ref[angle, brick], count)
-            for tile in range(count):
+            moved = shift_tiles(pieces, OFFMAX - offset_ref[angle, brick], z.half)
+            for tile in range(z.half):
                 rows = pl.ds((tile * z.angles + angle) * SUB, SUB)
                 sum_ref[rows, :] = sum_ref[rows, :] + moved[tile]
 
@@ -205,13 +225,12 @@
     column = me * z.band - z.left + lane
     inside = (column >= 0) & (column < z.columns)
     for row in range(z.layers + 1):
-        total = -jnp.concatenate(
-            [
-                sum_ref[pl.ds(tile * z.angles * SUB + row, z.angles, SUB), :]
-                for tile in range(z.width_p // LANES)
-            ],
-            axis=1,
-        )
+        parts = []
+        for tile in range(count):
+            place, segment = tile % z.half, tile // z.half
+            at = place * z.angles * SUB + segment * 4 + row
+            parts.append(sum_ref[pl.ds(at, z.angles, SUB), :])
+        total = -jnp.concatenate(parts, axis=1)
         if row < z.layers:
             window = own_ref[row]
             order = 0
@@ -232,43 +251,66 @@
 
 
 def adjoint_kernel(z, message_ref, sine_ref, cosine_ref, out_ref):
-    inner = z.layers * z.tap_lanes
+    inner = z.near_layers * z.tap_lanes
+    tiles = -(-inner // LANES)
+    masks = []
+    for tile in range(tiles):
+        layer = (tile * LANES + lane_index((SUB, LANES))) // z.tap_lanes
+        row = lax.broadcasted_iota(jnp.int32, (SUB, LANES), 0)
+        masks.append((row == layer, row == layer + 1))
 
     def brick_step(brick):
         taps = tap_rows(z, message_ref, brick)
-        rise = 0.5 + 0.45 * sine_ref[:, :LANES] * cosine_ref[brick, :, :LANES]
-        spread = spread_rows(z, taps * (1.0 - rise), taps * rise)
-        high, low = split(spread.T[:inner])
+        rise = 0.5 + 0.45 * sine_ref[...] * cosine_ref[brick]
+        low, high = taps * (1.0 - rise), taps * rise
+        columns = []
+        for same, above in masks:
+            blocks = []
+            for angle in range(z.angles):
+                first = jnp.broadcast_to(low[angle : angle + 1], (SUB, LANES))
+                second = jnp.broadcast_to(high[angle : angle + 1], (SUB, LANES))
+                blocks.append(jnp.where(same, first, jnp.where(above, second, 0.0)))
+            columns.append(jnp.concatenate(blocks, axis=0).T)
+        high, low = split(jnp.concatenate(columns, axis=0)[:inner])
         out_ref[brick] = jnp.concatenate([high, low, high], axis=1).astype(jnp.bfloat16)
 
     for_bricks(z, brick_step)
 
 
-def backproject_kernel(z, place_ref, offset_ref, own_ref, near_ref, far_ref, message_ref, weight_ref, out_ref, row_ref):
+def finish_kernel(z, place_ref, offset_ref, own_ref, near_ref, far_ref, message_ref, near_volume_ref, far_volume_ref, weight_ref, *refs):
+    *skip_refs, out_ref, row_ref, field_ref = refs
+    height_of = place_ref[1]
+    even = height_of % 2 == 0
+    lower_pair = height_of % 4 < 2
     row_ref[...] = jnp.zeros_like(row_ref)
-    last = place_ref[1] == z.height - 1
-    even = place_ref[1] % 2 == 0
-    below = jnp.where(even, far_ref[...], near_ref[...])
-    above = jnp.where(even, near_ref[...], far_ref[...])
-    for row in range(z.layers + 1):
-        value = own_ref[row]
-        if row == 0:
-            value = value + below
-        if row == z.layers:
-            value = jnp.where(last, 0.0, value + above)
+    below = [jnp.where(even, far_ref[row], near_ref[row]) for row in range(z.layers + 1)]
+    above = [jnp.where(even, near_ref[row], far_ref[row]) for row in range(z.layers + 1)]
+    above_two = jnp.where(lower_pair, skip_refs[0][...], skip_refs[-1][...])
+    below_two = jnp.where(lower_pair, skip_refs[-1][...], skip_refs[0][...])
+    below_two = jnp.where(height_of >= 2, below_two, 0.0)
+    above_two = jnp.where(height_of + 2 < z.height, above_two, 0.0)
+    own = [own_ref[row] for row in range(z.layers + 1)]
+    own[0] = own[0] + jnp.where(height_of >= 1, below[z.layers], 0.0)
+    below[0] = below[0] + below_two
+    above_end = above_two + above[z.layers]
+    above[0] = above[0] + own[z.layers]
+    rows = below[: z.layers] + own[: z.layers] + above[: z.layers] + [above_end]
+    for index, value in enumerate(rows):
+        place = height_of * z.layers - z.margin + index
+        value = jnp.where((place >= 0) & (place < z.height * z.layers), value, 0.0)
         for tile in range(z.width_p // LANES):
-            row_ref[pl.ds(tile * z.angles * SUB + row, z.angles, SUB), :] = value[
+            row_ref[pl.ds(tile * z.angles * SUB + index, z.angles, SUB), :] = value[
                 :, tile * LANES : (tile + 1) * LANES
             ]
-    lead = z.vol_left - SWEEPS
-
+    start = z.lead - z.lag
     count = z.field_p // LANES
+    have = z.width_p // LANES
 
     def brick_step(brick):
         blocks = []
         for angle in range(z.angles):
             tiles = [
-                row_ref[pl.ds((tile * z.angles + angle) * SUB, SUB), :]
+                row_ref[pl.ds((min(tile, have - 1) * z.angles + angle) * SUB, SUB), :]
                 for tile in range(count + 1)
             ]
             moved = shift_tiles(tiles, OFFMAX + offset_ref[angle, brick], count)
@@ -281,50 +323,37 @@
             jnp.concatenate([high, high, low], axis=0),
             preferred_element_type=jnp.float32,
         )
-        for layer in range(z.layers):
+        for index in range(z.near_layers):
             update = None
             for tap in range(z.taps):
-                begin = (layer * z.taps + tap) * z.slices
-                term = roll_left(product[begin : begin + z.slices], tap)
+                begin = (index * z.taps + tap) * z.slices
+                term = roll_left(product[begin : begin + z.slices], tap - z.lag)
                 update = term if update is None else update + term
-            start = lead // LANES * LANES
-            voxels = message_ref[
-                brick, layer * z.slices : (layer + 1) * z.slices, start : start + z.field_p + LANES
-            ]
-            voxels = roll_left(voxels, lead - start)[:, : z.field_p]
-            out_ref[layer, brick] = voxels + relax_step * update
+            layer = index % z.layers
+            rows = pl.ds(layer * z.slices, z.slices)
+            if z.margin <= index < z.margin + z.layers:
+                voxels = message_ref[brick, rows, start : start + z.field_p]
+            else:
+                near, far = near_volume_ref[brick, rows, :], far_volume_ref[brick, rows, :]
+                voxels = jnp.where(even == (index >= z.margin), near, far)
+            field_ref[index, pl.ds(brick * z.slices, z.slices), :] = voxels + relax_step * update
 
     for_bricks(z, brick_step)
 
-
-def denoise_kernel(z, place_ref, near_ref, own_ref, far_ref, out_ref):
     shape = (z.total_slices, z.field_p)
-    column = place_ref[0] * z.band - SWEEPS + lane_index(shape)
+    column = place_ref[0] * z.band - SWEEPS - z.lag + lane_index(shape)
     slice_at = lax.broadcasted_iota(jnp.int32, shape, 0)
     allow_x = (column >= 0) & (column + 1 < z.columns)
     allow_y = slice_at + 1 < z.total_slices
     not_first = slice_at > 0
-    first_layer = place_ref[1] * z.layers
-    even = place_ref[1] % 2 == 0
-    values = {}
-    for layer in range(-SWEEPS, z.layers + SWEEPS):
-        if layer < 0:
-            values[layer] = jnp.where(
-                even, far_ref[z.layers + layer], near_ref[z.layers + layer]
-            )
-        elif layer < z.layers:
-            values[layer] = own_ref[layer]
-        else:
-            values[layer] = jnp.where(
-                even, near_ref[layer - z.layers], far_ref[layer - z.layers]
-            )
+    values = {index - z.margin: field_ref[index] for index in range(z.near_layers)}
     for sweep in range(SWEEPS):
         margin = SWEEPS - 1 - sweep
         later = {}
         before = None
         for layer in range(-margin - 1, z.layers + margin):
             here = values[layer]
-            place = first_layer + layer
+            place = height_of * z.layers + layer
             allow_z = (place >= 0) & (place + 1 < z.height * z.layers)
             along_z = jnp.where(allow_z, values[layer + 1] - here, 0.0)
             along_y = jnp.where(allow_y, pltpu.roll(here, z.total_slices - 1, 0) - here, 0.0)
@@ -348,7 +377,7 @@
             before = normal_z
         values = later
     for layer in range(z.layers):
-        result = roll_left(values[layer], SWEEPS)
+        result = roll_left(values[layer], SWEEPS + z.lag)
         for brick in range(z.depth):
             out_ref[brick, layer] = result[brick * z.slices : (brick + 1) * z.slices, : z.band]
 
@@ -359,12 +388,18 @@
     return lax.ppermute(value, axis, pairs)
 
 
-def swapped(value, axis, first):
-    count = lax.axis_size(axis)
+def swapped(value, first, step=1):
+    depth, height = lax.axis_size("depth"), lax.axis_size("height")
     pairs = []
-    for low in range(first, count - 1, 2):
-        pairs += [(low, low + 1), (low + 1, low)]
-    return lax.ppermute(value, axis, pairs)
+    for depth_at in range(depth):
+        for height_at in range(height):
+            partner = height_at + (step if (height_at - first) // step % 2 == 0 else -step)
+            source = depth_at * height + height_at
+            if 0 <= partner < height:
+                pairs.append((source, depth_at * height + partner))
+            elif depth_at ^ 1 < depth:
+                pairs.append((source, (depth_at ^ 1) * height + height_at))
+    return lax.ppermute(value, ("depth", "height"), pairs)
 
 
 def call(kernel, z, shape, specs, scratch=(), dtype=jnp.float32, limit=16 << 20):
@@ -396,12 +431,11 @@
         jnp.transpose(measured, (1, 0, 2)),
         ((0, 0), (0, 0), (z.left, z.width_p - z.left - z.band)),
     )
-    segment_lanes = up_to(3 * z.layers * z.tap_lanes, LANES)
     angle_value = 2.0 * math.pi / N_VIEWS * angle_index.astype(jnp.float32)
-    sine = jnp.broadcast_to(jnp.sin(angle_value)[:, None], (z.angles, segment_lanes))
+    sine = jnp.broadcast_to(jnp.sin(angle_value)[:, None], (z.angles, LANES))
     slice_at = (
         jnp.arange(z.depth, dtype=jnp.int32)[:, None] * z.slices
-        + jnp.arange(segment_lanes, dtype=jnp.int32)[None, :] % z.slices
+        + jnp.arange(LANES, dtype=jnp.int32)[None, :] % z.slices
     )
     cosine = jnp.cos(math.pi / z.total_slices * (slice_at.astype(jnp.float32) + 0.5))[:, None, :]
 
@@ -412,40 +446,47 @@
         jnp.transpose(taps, (0, 2, 1)).reshape(z.tap_lanes, z.angles),
     )
     message = lax.all_to_all(message, "depth", 0, 0)
+    start = z.lead - z.lag
+    voxels = message[:, :, start : start + z.field_p]
+    volume_far = swapped(voxels, 1)
+    volume_near = swapped(voxels, 0)
+    tiles = 2 * 3 * z.layers * z.tap_lanes // LANES
     partial = call(
         project_kernel,
         z,
         (z.layers + 1, z.angles, z.width_p),
         [SMEM, SMEM, VMEM, VMEM, VMEM, VMEM] + [VMEM] * len(pieces),
-        [pltpu.VMEM((z.width_p // LANES * z.angles * SUB, LANES), jnp.float32)],
+        [
+            pltpu.VMEM((z.half * z.angles * SUB, LANES), jnp.float32),
+            pltpu.VMEM((z.depth * 2 * tiles * z.angles + SUB, LANES), jnp.float32),
+        ],
     )(place, band_offset, message, own, sine, cosine, *pieces)
-    even = height_of % 2 == 0
+    lower_pair = height_of % 4 < 2
     upward, downward = partial[z.layers], partial[0]
-    far = swapped(jnp.where(even, downward, upward), "height", 1)
-    near = swapped(jnp.where(even, upward, downward), "height", 0)
+    far = swapped(partial, 1)
+    skips = [swapped(jnp.where(lower_pair, upward, downward), 0, 2)]
+    if z.height > 4:
+        skips.append(swapped(jnp.where(lower_pair, downward, upward), 2, 2))
+    near = swapped(partial, 0)
     weight = call(
         adjoint_kernel,
         z,
-        (z.depth, z.layers * z.tap_lanes, 3 * z.angles * SUB),
+        (z.depth, z.near_layers * z.tap_lanes, 3 * z.angles * SUB),
         [VMEM, VMEM, VMEM],
         dtype=jnp.bfloat16,
     )(message, sine, cosine)
-    field = call(
-        backproject_kernel,
-        z,
-        (z.layers, z.depth, z.slices, z.field_p),
-        [SMEM, SMEM, VMEM, VMEM, VMEM, VMEM, VMEM],
-        [pltpu.VMEM((z.width_p // LANES * z.angles * SUB, LANES), jnp.float32)],
-    )(place, band_offset, partial, near, far, message, weight)
-    field = field.reshape(z.layers, z.total_slices, z.field_p)
-    field_far = swapped(field, "height", 1)
-    field_near = swapped(field, "height", 0)
     bands = call(
-        denoise_kernel,
+        finish_kernel,
         z,
         (z.depth, z.layers, z.slices, z.band),
-        [SMEM, VMEM, VMEM, VMEM],
-    )(place, field_near, field, field_far)
+        [SMEM, SMEM] + [VMEM] * (7 + len(skips)),
+        [
+            pltpu.VMEM((z.width_p // LANES * z.angles * SUB, LANES), jnp.float32),
+            pltpu.VMEM((z.near_layers, z.total_slices, z.field_p), jnp.float32),
+        ],
+    )(
+        place, band_offset, partial, near, far, message, volume_near, volume_far, weight, *skips
+    )
     bands = lax.all_to_all(bands, "depth", 0, 0)
     return jnp.transpose(bands, (1, 2, 0, 3)).reshape(volume.shape)
 

time: 54.6 us -> 51.6 us (0.945)
  the two profiles are of different devices: /device:TPU:1 before, /device:TPU:0 now
where the time goes in v3:
time: 51.6 us; the launch traced here: 51.2 us
  starting transfers between devices  16.9 us (33%)
  waiting for transfers between devices  12.7 us (25%)
  blocking collectives  10.4 us (20%)
  Pallas kernels  8.29 us (16%)
  local copies, waits for them, and re-layouts  2.59 us (5%)
    all_to_all x1, blocking collectives, per_device(): bands = lax.all_to_all(bands, 'depth', 0, 0)  10.4 us
    all_to_all x1, waiting for transfers between devices, per_device(): message = lax.all_to_all(message, 'depth', 0, 0)  9.18 us
    ppermute x2, starting transfers between devices, shifted(): return lax.ppermute(value, axis, pairs)  6.82 us
    all_to_all x1, starting transfers between devices, per_device(): message = lax.all_to_all(message, 'depth', 0, 0)  6.22 us
    ppermute x5, starting transfers between devices, swapped(): return lax.ppermute(value, ('depth', 'height'), pairs)  3.85 us
    pallas_call x1, Pallas kernels, per_device(): call(finish_kernel, z, (z.depth, z.layers, z.slices, z.band), [SMEM, SMEM...  3.64 us
    ppermute x5, waiting for transfers between devices, swapped(): return lax.ppermute(value, ('depth', 'height'), pairs)  3.5 us
    pallas_call x1, Pallas kernels, per_device(): call(project_kernel, z, (z.layers + 1, z.angles, z.width_p), [SMEM, SMEM,...  2.1 us
  transfers between devices with their start and end apart: 8, of which 2 were waited for; matrix products, arithmetic and copies ran while one was open for 3% of the time, Pallas kernels for 5%

profile of v3, /device:TPU:0, one launch (start us, length us, event | category | flops | bytes accessed | tf_op | source)
XLA Modules:
  0.0 51.2 jit_solution(4610225181537056792)
XLA Ops:
  0.0 0.8 %slice_bitcast_fusion.1 = f32[2,16,69]{2,0,1:T(2,128)S(1)} fusion(f32[16,2,256]{2,1,0:T(2,128)} %param.6), kind=kLoop, calls=%fused_computation.4 | loop fusion | bytes 17664 | tf_op jit(solution)/shard_map/transpose | solution.py:426
  0.8 1.3 %collective-permute-start = (f32[32,128]{1,0:T(8,128)S(1)}, f32[32,128]{1,0:T(8,128)S(1)}, u32[]{:S(2)}, u32[]{:S(2)}) collective-permute-start(f32[32,128]{1,0:T(8,128)S(1)} %bitcast.24), channel_id=1, source_target_pairs={{4,0},{8,4},{12,8},{16,12},{20,16},{24,20},{28,24},{5,1},{9,5},{13... | collective-permute-start | bytes 49160 | tf_op jit(solution)/shard_map/ppermute | solution.py:388
  2.1 0.8 %slice_bitcast_fusion = f32[2,16,66]{2,0,1:T(2,128)S(1)} fusion(f32[16,2,256]{2,1,0:T(2,128)} %param.6), kind=kLoop, calls=%fused_computation.3 | loop fusion | bytes 16896 | tf_op jit(solution)/shard_map/transpose | solution.py:426
  2.9 5.5 %collective-permute-start.1 = (f32[32,128]{1,0:T(8,128)S(1)}, f32[32,128]{1,0:T(8,128)S(1)}, u32[]{:S(2)}, u32[]{:S(2)}) collective-permute-start(f32[32,128]{1,0:T(8,128)S(1)} %bitcast.25), channel_id=1, source_target_pairs={{0,4},{4,8},{8,12},{12,16},{16,20},{20,24},{24,28},{1,5},{5,9},{9,... | collective-permute-start | bytes 49160 | tf_op jit(solution)/shard_map/ppermute | solution.py:388
  8.5 1.8 %shard_map.55 = f32[8,16,640]{2,1,0:T(8,128)} custom-call(f32[16,2048]{1,0:T(8,128)} %bitcast.23, f32[32,16]{1,0:T(8,128)} %bitcast.27), custom_call_target="tpu_custom_call" | custom-call | tf_op jit(solution)/shard_map/pallas_call | solution.py:442
  10.2 6.2 %all-to-all-start = ((f32[8,16,640]{2,1,0:T(8,128)}), f32[8,16,640]{2,1,0:T(8,128)S(1)}, u32[]{:S(2)}, u32[]{:S(2)}) async-start(f32[8,16,640]{2,1,0:T(8,128)} %shard_map.55), calls=%async_computation | async-start | bytes 655360 | tf_op jit(solution)/shard_map/all_to_all | solution.py:448
  16.5 0.1 add.64
  16.6 0.1 multiply_cosine_fusion.refs_5_.refs_2_
  16.7 0.1 pad_add_fusion.refs_0_
  16.8 0.1 copy.22.refs_1_
  16.9 0.1 pad.12.refs_3_
  17.0 0.0 collective-permute-done.refs_6_
  17.0 9.2 %all-to-all-done.refs_2_.refs_0_.refs_5_ = f32[8,16,640]{2,1,0:T(8,128)S(1)} async-done(((f32[8,16,640]{2,1,0:T(8,128)}), f32[8,16,640]{2,1,0:T(8,128)S(1)}, u32[]{:S(2)}, u32[]{:S(2)}) %all-to-all-start) | async-done | bytes 327712 | tf_op jit(solution)/shard_map/all_to_all | solution.py:448
  26.2 0.1 broadcast_in_dim.2.refs_4_.refs_1_
  26.2 2.1 %shard_map.56.refs_2_ = f32[3,16,512]{2,1,0:T(8,128)S(1)} custom-call(s32[2]{0:T(128)S(1)} %pad_add_fusion.refs_0_, s32[16,8]{1,0:T(8,128)S(1)} %copy.22.refs_1_, f32[8,16,640]{2,1,0:T(8,128)S(1)} %all-to-all-done.refs_2_.refs_0_.refs_5_, f32[2,16,512]{2,1,0:T(8,128)S(1)} %pad.12.refs_3_, f32[16,128]{1,0:T(8,128)S(1)} %broadcast_in_dim.2.refs_4_.refs_1_, ...), custom_call_target="tpu_custom_call" | custom-call | tf_op jit(solution)/shard_map/pallas_call | solution.py:454
  28.3 1.6 %collective-permute-start.3 = (f32[3,16,512]{2,1,0:T(8,128)S(1)}, f32[3,16,512]{2,1,0:T(8,128)S(1)}, u32[]{:S(2)}, u32[]{:S(2)}) collective-permute-start(f32[3,16,512]{2,1,0:T(8,128)S(1)} %shard_map.56.refs_2_), channel_id=1, source_target_pairs={{0,4},{1,2},{2,1},{3,7},{4,0},{5,6},{6,5},{7,3},{8,12},{9,10},{10,... | collective-permute-start | bytes 294920 | tf_op jit(solution)/shard_map/ppermute | solution.py:402
  29.9 0.1 collective-permute-start.2
  30.0 1.6 %collective-permute-start.5 = (f32[8,16,384]{2,1,0:T(8,128)S(1)}, f32[8,16,384]{2,1,0:T(8,128)S(1)}, u32[]{:S(2)}, u32[]{:S(2)}) collective-permute-start(f32[8,16,384]{2,1,0:T(8,128)S(1)} %slice.20), channel_id=1, source_target_pairs={{0,4},{1,2},{2,1},{3,7},{4,0},{5,6},{6,5},{7,3},{8,12},{9,10},{10,... | collective-permute-start | bytes 589832 | tf_op jit(solution)/shard_map/ppermute | solution.py:402
  31.6 0.6 %collective-permute-start.6 = (f32[16,512]{1,0:T(8,128)S(1)}, f32[16,512]{1,0:T(8,128)S(1)}, u32[]{:S(2)}, u32[]{:S(2)}) collective-permute-start(f32[16,512]{1,0:T(8,128)S(1)} %fusion), channel_id=1, source_target_pairs={{0,2},{1,3},{2,0},{3,1},{4,6},{5,7},{6,4},{7,5},{8,10},{9,11},{10,... | collective-permute-start | bytes 98312 | tf_op jit(solution)/shard_map/ppermute | solution.py:402
  32.2 0.8 %shard_map.57.refs_8_ = bf16[8,192,384]{2,1,0:T(8,128)(2,1)S(1)} custom-call(f32[8,16,640]{2,1,0:T(8,128)S(1)} %all-to-all-done.refs_2_.refs_0_.refs_5_, f32[16,128]{1,0:T(8,128)S(1)} %broadcast_in_dim.2.refs_4_.refs_1_, f32[8,1,128]{2,1,0:T(1,128)S(1)} %multiply_cosine_fusion.refs_5_.refs_2_), custom_call_target="tpu_custom_call" | custom-call | tf_op jit(solution)/shard_map/pallas_call | solution.py:471
  33.0 3.5 %collective-permute-done.6.refs_9_ = f32[16,512]{1,0:T(8,128)S(1)} collective-permute-done((f32[16,512]{1,0:T(8,128)S(1)}, f32[16,512]{1,0:T(8,128)S(1)}, u32[]{:S(2)}, u32[]{:S(2)}) %collective-permute-start.6) | collective-permute-done | bytes 32800 | tf_op jit(solution)/shard_map/ppermute | solution.py:402
  36.5 3.6 %shard_map.58 = f32[8,2,8,256]{3,2,1,0:T(8,128)S(1)} custom-call(s32[2]{0:T(128)S(1)} %pad_add_fusion.refs_0_, s32[16,8]{1,0:T(8,128)S(1)} %copy.22.refs_1_, f32[3,16,512]{2,1,0:T(8,128)S(1)} %shard_map.56.refs_2_, f32[3,16,512]{2,1,0:T(8,128)S(1)} %collective-permute-done.2.refs_3_, f32[3,16,512]{2,1,0:T(8,128)S(1)} %collective-permute-done.3.refs_4_, ...), custom_call_target="tpu_custom_call" | custom-call | tf_op jit(solution)/shard_map/pallas_call | solution.py:478
  40.2 10.4 %all_to_all.10 = f32[8,2,8,256]{3,2,1,0:T(8,128)S(1)} all-to-all(f32[8,2,8,256]{3,2,1,0:T(8,128)S(1)} %shard_map.58), channel_id=1, replica_groups=mesh['depth'=8,'height'=4] {'depth'}, dimensions={0} | all-to-all | bytes 262144 | tf_op jit(solution)/shard_map/all_to_all | solution.py:490
  50.5 0.7 %copy.26 = f32[8,2,1,8,256]{4,3,0,2,1:T(8,128)} copy(f32[8,2,1,8,256]{4,3,2,1,0:T(8,128)S(1)} %bitcast.21) | data formatting | bytes 262144 | tf_op jit(solution)/shard_map/reshape | solution.py:491
  (22 shorter events, 0.1 us)
Async XLA Ops:
  0.0 16.8 %copy-start = (f32[16,2,256]{2,1,0:T(2,128)S(1)}, f32[16,2,256]{2,1,0:T(2,128)}, u32[]{:S(2)}) copy-start(f32[16,2,256]{2,1,0:T(2,128)} %param.6) | copy-start | bytes 98308
  0.0 16.5 %copy-start.2 = (s32[16]{0:T(128)S(1)}, s32[16]{0:T(128)}, u32[]{:S(2)}) copy-start(s32[16]{0:T(128)} %param.9) | copy-start | bytes 196
  0.0 16.8 %copy-start.1 = (s32[16,8]{0,1:T(8,128)S(1)}, s32[16,8]{0,1:T(8,128)}, u32[]{:S(2)}) copy-start(s32[16,8]{0,1:T(8,128)} %param.8) | copy-start | bytes 1540
  0.8 16.2 %collective-permute-start = (f32[32,128]{1,0:T(8,128)S(1)}, f32[32,128]{1,0:T(8,128)S(1)}, u32[]{:S(2)}, u32[]{:S(2)}) collective-permute-start(f32[32,128]{1,0:T(8,128)S(1)} %bitcast.24), channel_id=1, source_target_pairs={{4,0},{8,4},{12,8},{16,12},{20,16},{24,20},{28,24},{5,1},{9,5},{13... | collective-permute-start | bytes 49160 | tf_op jit(solution)/shard_map/ppermute | solution.py:388
  2.9 14.1 %collective-permute-start.1 = (f32[32,128]{1,0:T(8,128)S(1)}, f32[32,128]{1,0:T(8,128)S(1)}, u32[]{:S(2)}, u32[]{:S(2)}) collective-permute-start(f32[32,128]{1,0:T(8,128)S(1)} %bitcast.25), channel_id=1, source_target_pairs={{0,4},{4,8},{8,12},{12,16},{16,20},{20,24},{24,28},{1,5},{5,9},{9,... | collective-permute-start | bytes 49160 | tf_op jit(solution)/shard_map/ppermute | solution.py:388
  10.2 15.9 %all-to-all-start = ((f32[8,16,640]{2,1,0:T(8,128)}), f32[8,16,640]{2,1,0:T(8,128)S(1)}, u32[]{:S(2)}, u32[]{:S(2)}) async-start(f32[8,16,640]{2,1,0:T(8,128)} %shard_map.55), calls=%async_computation | async-start | bytes 655360 | tf_op jit(solution)/shard_map/all_to_all | solution.py:448
  28.3 8.1 %collective-permute-start.3 = (f32[3,16,512]{2,1,0:T(8,128)S(1)}, f32[3,16,512]{2,1,0:T(8,128)S(1)}, u32[]{:S(2)}, u32[]{:S(2)}) collective-permute-start(f32[3,16,512]{2,1,0:T(8,128)S(1)} %shard_map.56.refs_2_), channel_id=1, source_target_pairs={{0,4},{1,2},{2,1},{3,7},{4,0},{5,6},{6,5},{7,3},{8,12},{9,10},{10,... | collective-permute-start | bytes 294920 | tf_op jit(solution)/shard_map/ppermute | solution.py:402
  29.9 6.6 %collective-permute-start.2 = (f32[3,16,512]{2,1,0:T(8,128)S(1)}, f32[3,16,512]{2,1,0:T(8,128)S(1)}, u32[]{:S(2)}, u32[]{:S(2)}) collective-permute-start(f32[3,16,512]{2,1,0:T(8,128)S(1)} %shard_map.56.refs_2_), channel_id=1, source_target_pairs={{0,1},{1,0},{2,3},{3,2},{4,5},{5,4},{6,7},{7,6},{8,9},{9,8},{10,11... | collective-permute-start | bytes 294920 | tf_op jit(solution)/shard_map/ppermute | solution.py:402
  30.0 6.5 %collective-permute-start.5 = (f32[8,16,384]{2,1,0:T(8,128)S(1)}, f32[8,16,384]{2,1,0:T(8,128)S(1)}, u32[]{:S(2)}, u32[]{:S(2)}) collective-permute-start(f32[8,16,384]{2,1,0:T(8,128)S(1)} %slice.20), channel_id=1, source_target_pairs={{0,4},{1,2},{2,1},{3,7},{4,0},{5,6},{6,5},{7,3},{8,12},{9,10},{10,... | collective-permute-start | bytes 589832 | tf_op jit(solution)/shard_map/ppermute | solution.py:402
  31.6 4.9 %collective-permute-start.4 = (f32[8,16,384]{2,1,0:T(8,128)S(1)}, f32[8,16,384]{2,1,0:T(8,128)S(1)}, u32[]{:S(2)}, u32[]{:S(2)}) collective-permute-start(f32[8,16,384]{2,1,0:T(8,128)S(1)} %slice.20), channel_id=1, source_target_pairs={{0,1},{1,0},{2,3},{3,2},{4,5},{5,4},{6,7},{7,6},{8,9},{9,8},{10,11... | collective-permute-start | bytes 589832 | tf_op jit(solution)/shard_map/ppermute | solution.py:402
  31.6 4.9 %collective-permute-start.6 = (f32[16,512]{1,0:T(8,128)S(1)}, f32[16,512]{1,0:T(8,128)S(1)}, u32[]{:S(2)}, u32[]{:S(2)}) collective-permute-start(f32[16,512]{1,0:T(8,128)S(1)} %fusion), channel_id=1, source_target_pairs={{0,2},{1,3},{2,0},{3,1},{4,6},{5,7},{6,4},{7,5},{8,10},{9,11},{10,... | collective-permute-start | bytes 98312 | tf_op jit(solution)/shard_map/ppermute | solution.py:402
